TPU v7x, 128 devices: a whole 4x4x4 slice. The times are simulated.
128 devices in a mesh: cam: 8 (over z, core), ray: 16 (over y, x).
Axes of the slice: x: 4, y: 4, z: 4, core: 2. Of those that a mesh axis runs over, the one named last changes fastest.
Arguments:
- encodings: bfloat16 [8192, 48, 128], P(('cam', 'ray')), may hold values from -6 to 6
- ray_camera: int32 [8192], P(('cam', 'ray')), may hold values from 0 to 32767, as said below
- targets: float32 [8192, 3], P(('cam', 'ray')), may hold values from -6 to 6
- weights: bfloat16 [4, 128, 128], replicated, may hold values from -0.5 to 0.5
- head_weight: bfloat16 [128, 3], replicated, may hold values from -0.5 to 0.5
- quadrature: float32 [48], replicated, may hold values from 0.05 to 0.3
- lift: float32 [38, 128], replicated, may hold values from -1 to 1
- cam_params: float32 [38, 32768], P(None, ('cam', 'ray')), may hold values from -6 to 6
- damping: float32 [38, 32768], P(None, ('cam', 'ray')), may hold values from 1 to 30
Outputs:
- update: float32 [38, 32768], P(None, ('cam', 'ray'))
- cg_residual: float32 [38, 32768], P(None, ('cam', 'ray'))
Inputs may be any that keep to these rules, and one draw needn't show every extreme that they name: ray_camera is the same for all 64 rays of each aligned block of 64 rays.
All inputs are finite; a program needn't handle non-finite values.
Results may differ from a plain program's by a relative error of at most 0.008.
Values sent between devices are 32-bit elements; how exact they have to be, the bound alone decides.
A program may use at most 64 MiB of HBM per device.

v0:
```python
import jax
import jax.numpy as jnp
from jax import lax
from jax.sharding import Mesh
from jax.sharding import PartitionSpec as P

BLOCK = 64
CG_ITERS = 2
CAM_RAY = ("cam_0", "cam_1", "ray_0", "ray_1")


precise = lax.Precision.HIGHEST


def sent_to_all(array, axis):
    copies = jnp.broadcast_to(array, (lax.axis_size(axis), *array.shape))
    return lax.all_to_all(copies, axis, split_axis=0, concat_axis=0, tiled=True)


def taken_together(array, axis):
    everything = sent_to_all(array, axis)
    return jnp.sum(everything, axis=0)


def one_axis_at_a_time(array, axes):
    far, near = axes
    nearer = taken_together(array, near)
    return taken_together(nearer, far)


def packed_total(arrays, axis):
    line, at, outs = (jnp.concatenate([a.reshape(-1) for a in arrays]), 0, [])
    running = one_axis_at_a_time(line, axis)
    for a in arrays:
        outs.append(running[at : at + a.size].reshape(a.shape))
        at += a.size
    return tuple(outs)


def joined_along(tiles, dim):
    tiles = jnp.moveaxis(tiles, 0, dim)
    shape = tiles.shape
    return tiles.reshape(*shape[:dim], shape[dim] * shape[dim + 1], *shape[dim + 2 :])


def whole_of(array, axes, dim):
    far, near = axes
    tiles = sent_to_all(sent_to_all(array, far), near)
    return joined_along(tiles.swapaxes(0, 1).reshape(-1, *array.shape), dim)


def cut_along(array, dim, peers):
    shape = array.shape
    tiles = array.reshape(*shape[:dim], peers, shape[dim] // peers, *shape[dim + 1 :])
    return jnp.moveaxis(tiles, dim, 0)


def sum_at_owner(array, axis, dim):
    tiles = cut_along(array, dim, lax.axis_size(axis))
    arrived = lax.all_to_all(tiles, axis, split_axis=0, concat_axis=0, tiled=True)
    return arrived.sum(axis=0)


def sum_by_axis(array, axes, dim):
    far, near = axes
    tiles = cut_along(array, dim, lax.axis_size(far))
    nearer = sum_at_owner(tiles, near, dim + 1)
    arrived = lax.all_to_all(nearer, far, split_axis=0, concat_axis=0, tiled=True)
    return arrived.sum(axis=0)


def forward(enc_group, lifted, weights, depths):
    row_count, sample_count, feature_width = enc_group.shape
    inner = enc_group.astype(jnp.float32) + depths[None, :, None] * lifted[:, None, :]
    layer_out = jnp.tanh(inner).astype(jnp.bfloat16)
    outputs = [layer_out]
    for layer in range(weights.shape[0]):
        inner = jnp.dot(
            layer_out.reshape(row_count * sample_count, feature_width),
            weights[layer],
            preferred_element_type=jnp.float32,
        )
        layer_out = (
            jnp.tanh(inner).astype(jnp.bfloat16).reshape(row_count, sample_count, feature_width)
        )
        outputs.append(layer_out)
    return outputs


def render(layer_out, head_weight, quadrature):
    mixed = jnp.sum(quadrature[None, :, None] * layer_out.astype(jnp.float32), axis=1)
    return jnp.dot(mixed, head_weight.astype(jnp.float32), precision=precise)


def tangent_pass(outputs, spread, weights, head_weight, quadrature, depths):
    row_count, sample_count, feature_width = outputs[0].shape
    slope = 1.0 - outputs[0].astype(jnp.float32) ** 2
    tangent = (slope * depths[None, :, None] * spread[:, None, :]).astype(jnp.bfloat16)
    for layer in range(weights.shape[0]):
        inner = jnp.dot(
            tangent.reshape(row_count * sample_count, feature_width),
            weights[layer],
            preferred_element_type=jnp.float32,
        )
        slope = 1.0 - outputs[layer + 1].astype(jnp.float32) ** 2
        tangent = (slope * inner.reshape(row_count, sample_count, feature_width)).astype(
            jnp.bfloat16
        )
    return render(tangent, head_weight, quadrature)


def adjoint_pass(outputs, pixel_grad, weights, head_weight, quadrature, depths):
    row_count, sample_count, feature_width = outputs[0].shape
    cotangent = jnp.dot(pixel_grad, head_weight.astype(jnp.float32).T, precision=precise)
    slope = 1.0 - outputs[-1].astype(jnp.float32) ** 2
    adjoint = (slope * quadrature[None, :, None] * cotangent[:, None, :]).astype(jnp.bfloat16)
    for layer in reversed(range(weights.shape[0])):
        inner = jnp.dot(
            adjoint.reshape(row_count * sample_count, feature_width),
            weights[layer].T,
            preferred_element_type=jnp.float32,
        )
        slope = 1.0 - outputs[layer].astype(jnp.float32) ** 2
        adjoint = (slope * inner.reshape(row_count, sample_count, feature_width)).astype(
            jnp.bfloat16
        )
    return jnp.sum(depths[None, :, None] * adjoint.astype(jnp.float32), axis=1)


def paired_sums(remainder, image):
    return packed_total(
        (jnp.sum(remainder * remainder), jnp.sum(remainder * image)),
        ("cam_0", ("cam_1", "ray_0", "ray_1")),
    )


def body(
    encodings, ray_camera, targets, weights, head_weight, quadrature, lift, cam_params, damping
):
    row_count, sample_count, feature_width = encodings.shape
    block_count = row_count // BLOCK
    depths = (jnp.arange(sample_count).astype(jnp.float32) + 1.0) / sample_count
    block_cam = ray_camera.reshape(block_count, BLOCK)[:, 0]
    cam_dev = cam_params.shape[1]
    position = lax.axis_index(CAM_RAY)
    all_cams = whole_of(block_cam, (("cam_0", "cam_1", "ray_0"), "ray_1"), 0)
    local_ids = all_cams - position * cam_dev
    owned = (local_ids >= 0) & (local_ids < cam_dev)
    clipped = jnp.clip(local_ids, 0, cam_dev - 1)
    selector = ((clipped[:, None] == jnp.arange(cam_dev)[None, :]) & owned[:, None]).astype(
        jnp.float32
    )

    def fetch_columns(values):
        answers = jnp.where(owned[None, :], values[:, clipped], 0.0)
        return sum_by_axis(answers, (("cam_0", "cam_1", "ray_0"), "ray_1"), 1)

    def collect_grads(grads):
        everything = whole_of(grads, (("cam_0", "cam_1", "ray_0"), "ray_1"), 1)
        return jnp.dot(everything, selector, precision=precise)

    def spread_rays(values):
        lifted = jnp.dot(lift.T, fetch_columns(values), precision=precise)
        return jnp.repeat(lifted.T, BLOCK, axis=0)

    def sum_to_cameras(ray_grads):
        summed = ray_grads.reshape(block_count, BLOCK, feature_width).sum(axis=1)
        return collect_grads(jnp.dot(lift, summed.T, precision=precise))

    outputs = forward(encodings, spread_rays(cam_params), weights, depths)
    residual_rays = render(outputs[-1], head_weight, quadrature) - targets
    right_side = -sum_to_cameras(
        adjoint_pass(outputs, residual_rays, weights, head_weight, quadrature, depths)
    )

    def operator(vector):
        image_rays = tangent_pass(
            outputs, spread_rays(vector), weights, head_weight, quadrature, depths
        )
        return (
            sum_to_cameras(
                adjoint_pass(outputs, image_rays, weights, head_weight, quadrature, depths)
            )
            + damping * vector
        )

    solution = jnp.zeros_like(right_side)
    remainder = right_side
    image = operator(remainder)
    norm_now, product = paired_sums(remainder, image)
    step_size = norm_now / product
    direction, along = (remainder, image)
    for step_index in range(CG_ITERS):
        solution = solution + step_size * direction
        remainder = remainder - step_size * along
        if step_index + 1 < CG_ITERS:
            image = operator(remainder)
            norm_next, product = paired_sums(remainder, image)
            ratio_next = norm_next / norm_now
            step_size = norm_next / (product - ratio_next * norm_next / step_size)
            direction = remainder + ratio_next * direction
            along = image + ratio_next * along
            norm_now = norm_next
    return (solution, remainder)


def solution(mesh):
    split = Mesh(mesh.devices.reshape(4, 2, 4, 4), ("cam_0", "cam_1", "ray_0", "ray_1"))
    in_specs = (
        P(CAM_RAY, None, None),
        P(CAM_RAY),
        P(CAM_RAY, None),
        P(),
        P(),
        P(),
        P(),
        P(None, CAM_RAY),
        P(None, CAM_RAY),
    )
    out_specs = (P(None, CAM_RAY), P(None, CAM_RAY))
    return jax.shard_map(body, mesh=split, in_specs=in_specs, out_specs=out_specs, check_vma=False)
```

profile of v0, /device:TPU:1, one launch (start us, length us, event | category | flops | bytes accessed | tf_op | source)
XLA Modules:
  0.0 242.2 jit_solution(4821253244868260728)
XLA Ops:
  0.7 1.3 broadcast_in_dim.44
  2.0 9.6 %all-to-all-start = ((s32[32,1,1]{2,1,0:T(1,128)}), s32[32,1,1]{2,1,0:T(1,128)S(1)}, u32[]{:S(2)}, u32[]{:S(2)}) async-start(s32[32,1,1]{2,1,0:T(1,128)} %broadcast_in_dim.44), calls=%async_computation | async-start | bytes 32768 | tf_op jit(solution)/shard_map/all_to_all | solution.py:17
  11.6 0.9 copy.76
  12.5 6.0 %all-to-all-done = s32[32,1,1]{2,1,0:T(1,128)S(1)} async-done(((s32[32,1,1]{2,1,0:T(1,128)}), s32[32,1,1]{2,1,0:T(1,128)S(1)}, u32[]{:S(2)}, u32[]{:S(2)}) %all-to-all-start) | async-done | bytes 160 | tf_op jit(solution)/shard_map/all_to_all | solution.py:17
  19.7 4.0 %all-to-all-start.1 = ((s32[4,32,1]{1,2,0:T(1,128)}), s32[4,32,1]{1,2,0:T(1,128)S(1)}, u32[]{:S(2)}, u32[]{:S(2)}) async-start(s32[4,32,1]{1,2,0:T(1,128)} %broadcast_in_dim.45), calls=%async_computation.1 | async-start | bytes 4096 | tf_op jit(solution)/shard_map/all_to_all | solution.py:17
  23.7 4.1 %all-to-all-done.1 = s32[4,32,1]{1,2,0:T(1,128)S(1)} async-done(((s32[4,32,1]{1,2,0:T(1,128)}), s32[4,32,1]{1,2,0:T(1,128)S(1)}, u32[]{:S(2)}, u32[]{:S(2)}) %all-to-all-start.1) | async-done | bytes 544 | tf_op jit(solution)/shard_map/all_to_all | solution.py:17
  28.9 6.6 %all_to_all.107 = f32[4,1,1216]{2,1,0:T(1,128)S(1)} all-to-all(f32[4,1,1216]{2,1,0:T(1,128)S(1)} %reshape.376), channel_id=1, replica_groups=mesh['cam_0'=4,'cam_1'=2,'ray_0'=4,'ray_1'=4] {'ray_1'}, dimensions={0} | all-to-all | bytes 38912 | tf_op jit(solution)/shard_map/all_to_all | solution.py:60
  37.6 6.7 %all-to-all-start.3 = ((f32[32,38,1]{1,2,0:T(1,128)}), f32[32,38,1]{1,2,0:T(1,128)S(1)}, u32[]{:S(2)}, u32[]{:S(2)}) async-start(f32[32,38,1]{1,2,0:T(1,128)} %bitcast.10), calls=%async_computation.3 | async-start | bytes 32768 | tf_op jit(solution)/shard_map/all_to_all | solution.py:68
  45.1 6.2 %all-to-all-done.3 = f32[32,38,1]{1,2,0:T(1,128)S(1)} async-done(((f32[32,38,1]{1,2,0:T(1,128)}), f32[32,38,1]{1,2,0:T(1,128)S(1)}, u32[]{:S(2)}, u32[]{:S(2)}) %all-to-all-start.3) | async-done | bytes 4896 | tf_op jit(solution)/shard_map/all_to_all | solution.py:68
  51.8 1.5 multiply_subtract_fusion.3
  53.3 1.5 multiply_subtract_fusion.2
  56.5 1.4 fusion.7
  57.9 3.2 %multiply_convert_fusion.20 = bf16[64,48,128]{2,1,0:T(8,128)(2,1)} fusion(f32[64,48,128]{2,1,0:T(8,128)} %bitcast.280, f32[64,48,128]{2,1,0:T(8,128)S(1)} %bitcast.275, bf16[64,48,128]{2,1,0:T(8,128)(2,1)} %bitcast.292, bf16[4,128,128]{2,1,0:T(8,128)(2,1)S(1)} %copy-done.3), kind=kOutput, calls=%fused_computation.44 | convolution fusion | flops 202899456 | bytes 4784128 | tf_op jit(solution)/shard_map/dot_general | solution.py:118
  61.1 2.5 %multiply_reduce_fusion.4 = f32[128]{0:T(128)S(1)} fusion(f32[64,48,128]{2,1,0:T(8,128)} %bitcast.285, bf16[64,48,128]{2,1,0:T(8,128)(2,1)} %multiply_convert_fusion.20, bf16[64,48,128]{2,1,0:T(8,128)(2,1)} %copy-done.2, f32[48]{0:T(128)S(1)} %add_multiply_fusion, bf16[4,128,128]{2,1,0:T(8,128)(2,1)S(1)} %copy-done.3), kind=kOutput, calls=%fused_computation.41 | convolution fusion | flops 205258624 | bytes 3212288 | tf_op jit(solution)/shard_map/dot_general | solution.py:118
  63.8 10.7 %all_to_all.108 = f32[32,38,1]{1,2,0:T(1,128)S(1)} all-to-all(f32[32,38,1]{1,2,0:T(1,128)S(1)} %broadcast_in_dim.87), channel_id=1, replica_groups=mesh['cam_0'=4,'cam_1'=2,'ray_0'=4,'ray_1'=4] {'cam_0','cam_1','ray_0'}, dimensions={0} | all-to-all | bytes 9728 | tf_op jit(solution)/shard_map/all_to_all | solution.py:17
  75.3 3.3 %all-to-all-start.5 = ((f32[4,1,1216]{2,1,0:T(1,128)}), f32[4,1,1216]{2,1,0:T(1,128)S(1)}, u32[]{:S(2)}, u32[]{:S(2)}) async-start(f32[4,1,1216]{2,1,0:T(1,128)} %reshape.378), calls=%async_computation.5 | async-start | bytes 40960 | tf_op jit(solution)/shard_map/all_to_all | solution.py:17
  78.9 3.9 %all-to-all-done.5 = f32[4,1,1216]{2,1,0:T(1,128)S(1)} async-done(((f32[4,1,1216]{2,1,0:T(1,128)}), f32[4,1,1216]{2,1,0:T(1,128)S(1)}, u32[]{:S(2)}, u32[]{:S(2)}) %all-to-all-start.5) | async-done | bytes 19488 | tf_op jit(solution)/shard_map/all_to_all | solution.py:17
  84.1 0.8 gather_fusion.1
  85.7 6.6 %all_to_all.109 = f32[4,1,1216]{2,1,0:T(1,128)S(1)} all-to-all(f32[4,1,1216]{2,1,0:T(1,128)S(1)} %reshape.380), channel_id=1, replica_groups=mesh['cam_0'=4,'cam_1'=2,'ray_0'=4,'ray_1'=4] {'ray_1'}, dimensions={0} | all-to-all | bytes 38912 | tf_op jit(solution)/shard_map/all_to_all | solution.py:60
  93.1 13.0 %all_to_all.110 = f32[32,38,1]{1,2,0:T(1,128)S(1)} all-to-all(f32[32,38,1]{1,2,0:T(1,128)S(1)} %bitcast.301), channel_id=1, replica_groups=mesh['cam_0'=4,'cam_1'=2,'ray_0'=4,'ray_1'=4] {'cam_0','cam_1','ray_0'}, dimensions={0} | all-to-all | bytes 9728 | tf_op jit(solution)/shard_map/all_to_all | solution.py:68
  106.3 3.7 %multiply_convert_fusion.15 = bf16[64,48,128]{2,1,0:T(8,128)(2,1)} fusion(f32[64,48,128]{2,1,0:T(8,128)} %bitcast.281, f32[64,48,128]{2,1,0:T(8,128)} %bitcast.286, bf16[64,48,128]{2,1,0:T(8,128)(2,1)} %copy-done.2, f32[128]{0:T(128)S(1)} %convolution_bitcast_fusion.3, f32[48]{0:T(128)} %copy-done.18, bf16[4,128,128]{2,1,0:T(8,128)(2,1)S(1)} %copy-done.3), kind=kOutput, calls=%fused_computation.37 | convolution fusion | flops 205258752 | bytes 4784832 | tf_op jit(solution)/shard_map/dot_general | solution.py:100
  110.0 1.8 multiply_reduce_fusion.3
  112.3 1.4 fusion.6
  113.6 3.2 %multiply_convert_fusion.11 = bf16[64,48,128]{2,1,0:T(8,128)(2,1)} fusion(f32[64,48,128]{2,1,0:T(8,128)} %bitcast.282, f32[64,48,128]{2,1,0:T(8,128)S(1)} %bitcast.277, bf16[64,48,128]{2,1,0:T(8,128)(2,1)} %bitcast.293, bf16[4,128,128]{2,1,0:T(8,128)(2,1)S(1)} %copy-done.3), kind=kOutput, calls=%fused_computation.32 | convolution fusion | flops 202899456 | bytes 4784128 | tf_op jit(solution)/shard_map/dot_general | solution.py:118
  116.9 2.5 %multiply_reduce_fusion.2 = f32[128]{0:T(128)S(1)} fusion(f32[64,48,128]{2,1,0:T(8,128)} %bitcast.287, bf16[64,48,128]{2,1,0:T(8,128)(2,1)} %multiply_convert_fusion.11, bf16[64,48,128]{2,1,0:T(8,128)(2,1)} %copy-done.2, f32[48]{0:T(128)S(1)} %copy-done.19, bf16[4,128,128]{2,1,0:T(8,128)(2,1)S(1)} %copy-done.3), kind=kOutput, calls=%fused_computation.29 | convolution fusion | flops 205258624 | bytes 3212288 | tf_op jit(solution)/shard_map/dot_general | solution.py:118
  119.6 10.7 %all_to_all.111 = f32[32,38,1]{1,2,0:T(1,128)S(1)} all-to-all(f32[32,38,1]{1,2,0:T(1,128)S(1)} %broadcast_in_dim.89), channel_id=1, replica_groups=mesh['cam_0'=4,'cam_1'=2,'ray_0'=4,'ray_1'=4] {'cam_0','cam_1','ray_0'}, dimensions={0} | all-to-all | bytes 9728 | tf_op jit(solution)/shard_map/all_to_all | solution.py:17
  130.4 6.6 %all_to_all.112 = f32[4,1,1216]{2,1,0:T(1,128)S(1)} all-to-all(f32[4,1,1216]{2,1,0:T(1,128)S(1)} %reshape.382), channel_id=1, replica_groups=mesh['cam_0'=4,'cam_1'=2,'ray_0'=4,'ray_1'=4] {'ray_1'}, dimensions={0} | all-to-all | bytes 38912 | tf_op jit(solution)/shard_map/all_to_all | solution.py:17
  137.9 1.6 multiply_reduce_fusion.9
  139.5 1.4 pad_maximum_fusion
  140.9 11.7 %all_to_all.113 = f32[32,1,2]{2,1,0:T(1,128)S(1)} all-to-all(f32[32,1,2]{2,1,0:T(1,128)S(1)} %broadcast_in_dim.91), channel_id=1, replica_groups=mesh['cam_0'=4,'cam_1'=2,'ray_0'=4,'ray_1'=4] {'cam_1','ray_0','ray_1'}, dimensions={0} | all-to-all | bytes 512 | tf_op jit(solution)/shard_map/all_to_all | solution.py:17
  152.7 6.5 %all_to_all.114 = f32[4,1,2]{2,1,0:T(1,128)S(1)} all-to-all(f32[4,1,2]{2,1,0:T(1,128)S(1)} %broadcast_in_dim.92), channel_id=1, replica_groups=mesh['cam_0'=4,'cam_1'=2,'ray_0'=4,'ray_1'=4] {'cam_0'}, dimensions={0} | all-to-all | bytes 64 | tf_op jit(solution)/shard_map/all_to_all | solution.py:17
  161.2 1.3 gather_fusion.2
  162.5 0.9 fusion.119
  163.6 6.6 %all_to_all.115 = f32[4,1,1216]{2,1,0:T(1,128)S(1)} all-to-all(f32[4,1,1216]{2,1,0:T(1,128)S(1)} %reshape.384), channel_id=1, replica_groups=mesh['cam_0'=4,'cam_1'=2,'ray_0'=4,'ray_1'=4] {'ray_1'}, dimensions={0} | all-to-all | bytes 38912 | tf_op jit(solution)/shard_map/all_to_all | solution.py:60
  170.2 0.7 reduce.24
  171.0 13.0 %all_to_all.116 = f32[32,38,1]{1,2,0:T(1,128)S(1)} all-to-all(f32[32,38,1]{1,2,0:T(1,128)S(1)} %bitcast.303), channel_id=1, replica_groups=mesh['cam_0'=4,'cam_1'=2,'ray_0'=4,'ray_1'=4] {'cam_0','cam_1','ray_0'}, dimensions={0} | all-to-all | bytes 9728 | tf_op jit(solution)/shard_map/all_to_all | solution.py:68
  184.3 3.8 %multiply_convert_fusion.6 = bf16[64,48,128]{2,1,0:T(8,128)(2,1)} fusion(f32[64,48,128]{2,1,0:T(8,128)} %bitcast.283, f32[64,48,128]{2,1,0:T(8,128)} %bitcast.288, bf16[64,48,128]{2,1,0:T(8,128)(2,1)} %copy-done.2, f32[128]{0:T(128)S(1)} %convolution_bitcast_fusion.1, f32[48]{0:T(128)} %copy-done.18, bf16[4,128,128]{2,1,0:T(8,128)(2,1)S(1)} %copy-done.3), kind=kOutput, calls=%fused_computation.26 | convolution fusion | flops 205258752 | bytes 4784832 | tf_op jit(solution)/shard_map/dot_general | solution.py:100
  188.0 1.8 multiply_reduce_fusion.1
  190.2 1.4 fusion.5
  191.6 3.3 %multiply_convert_fusion.2 = bf16[64,48,128]{2,1,0:T(8,128)(2,1)} fusion(f32[64,48,128]{2,1,0:T(8,128)} %bitcast.284, f32[64,48,128]{2,1,0:T(8,128)S(1)} %bitcast.279, bf16[64,48,128]{2,1,0:T(8,128)(2,1)} %bitcast.291, bf16[4,128,128]{2,1,0:T(8,128)(2,1)S(1)} %copy-done.3), kind=kOutput, calls=%fused_computation.21 | convolution fusion | flops 202899456 | bytes 4784128 | tf_op jit(solution)/shard_map/dot_general | solution.py:118
  195.0 2.1 multiply_reduce_fusion
  197.2 10.7 %all_to_all.117 = f32[32,38,1]{1,2,0:T(1,128)S(1)} all-to-all(f32[32,38,1]{1,2,0:T(1,128)S(1)} %broadcast_in_dim.93), channel_id=1, replica_groups=mesh['cam_0'=4,'cam_1'=2,'ray_0'=4,'ray_1'=4] {'cam_0','cam_1','ray_0'}, dimensions={0} | all-to-all | bytes 9728 | tf_op jit(solution)/shard_map/all_to_all | solution.py:17
  208.1 6.6 %all_to_all.118 = f32[4,1,1216]{2,1,0:T(1,128)S(1)} all-to-all(f32[4,1,1216]{2,1,0:T(1,128)S(1)} %reshape.386), channel_id=1, replica_groups=mesh['cam_0'=4,'cam_1'=2,'ray_0'=4,'ray_1'=4] {'ray_1'}, dimensions={0} | all-to-all | bytes 38912 | tf_op jit(solution)/shard_map/all_to_all | solution.py:17
  214.6 0.7 reduce.25
  215.6 1.0 multiply_reduce_fusion.7
  216.5 1.4 pad_maximum_fusion.1
  218.0 11.7 %all_to_all.119 = f32[32,1,2]{2,1,0:T(1,128)S(1)} all-to-all(f32[32,1,2]{2,1,0:T(1,128)S(1)} %broadcast_in_dim.95), channel_id=1, replica_groups=mesh['cam_0'=4,'cam_1'=2,'ray_0'=4,'ray_1'=4] {'cam_1','ray_0','ray_1'}, dimensions={0} | all-to-all | bytes 512 | tf_op jit(solution)/shard_map/all_to_all | solution.py:17
  229.8 6.5 %all_to_all.120 = f32[4,1,2]{2,1,0:T(1,128)S(1)} all-to-all(f32[4,1,2]{2,1,0:T(1,128)S(1)} %broadcast_in_dim.96), channel_id=1, replica_groups=mesh['cam_0'=4,'cam_1'=2,'ray_0'=4,'ray_1'=4] {'cam_0'}, dimensions={0} | all-to-all | bytes 64 | tf_op jit(solution)/shard_map/all_to_all | solution.py:17
  (128 shorter events, 16.6 us)
Async XLA Ops:
  0.6 50.7 %copy-start = (f32[38,128]{1,0:T(8,128)S(1)}, f32[38,128]{1,0:T(8,128)}, u32[]{:S(2)}) copy-start(f32[38,128]{1,0:T(8,128)} %param.15) | copy-start | bytes 58372
  0.6 50.8 %copy-start.4 = (bf16[64,48,128]{2,1,0:T(8,128)(2,1)S(1)}, bf16[64,48,128]{2,1,0:T(8,128)(2,1)}, u32[]{:S(2)}) copy-start(bf16[64,48,128]{2,1,0:T(8,128)(2,1)} %param.9) | copy-start | bytes 2359300
  0.7 51.2 %copy-start.3 = (bf16[4,128,128]{2,1,0:T(8,128)(2,1)S(1)}, bf16[4,128,128]{2,1,0:T(8,128)(2,1)}, u32[]{:S(2)}) copy-start(bf16[4,128,128]{2,1,0:T(8,128)(2,1)} %param.12) | copy-start | bytes 393220
  2.0 16.5 %all-to-all-start = ((s32[32,1,1]{2,1,0:T(1,128)}), s32[32,1,1]{2,1,0:T(1,128)S(1)}, u32[]{:S(2)}, u32[]{:S(2)}) async-start(s32[32,1,1]{2,1,0:T(1,128)} %broadcast_in_dim.44), calls=%async_computation | async-start | bytes 32768 | tf_op jit(solution)/shard_map/all_to_all | solution.py:17
  19.7 8.1 %all-to-all-start.1 = ((s32[4,32,1]{1,2,0:T(1,128)}), s32[4,32,1]{1,2,0:T(1,128)S(1)}, u32[]{:S(2)}, u32[]{:S(2)}) async-start(s32[4,32,1]{1,2,0:T(1,128)} %broadcast_in_dim.45), calls=%async_computation.1 | async-start | bytes 4096 | tf_op jit(solution)/shard_map/all_to_all | solution.py:17
  27.8 25.5 %copy-start.12 = (pred[32,4,1]{0,1,2:T(4,128)(4,1)}, pred[32,4,1]{0,1,2:T(4,128)(4,1)S(1)}, u32[]{:S(2)}) copy-start(pred[32,4,1]{0,1,2:T(4,128)(4,1)S(1)} %copy.121) | copy-start | bytes 388
  28.1 25.3 %copy-start.17 = (s32[1024]{0:T(1024)}, s32[1024]{0:T(1024)S(1)}, u32[]{:S(2)}) copy-start(s32[1024]{0:T(1024)S(1)} %pad_clamp_fusion) | copy-start | bytes 12292
  37.6 13.7 %all-to-all-start.3 = ((f32[32,38,1]{1,2,0:T(1,128)}), f32[32,38,1]{1,2,0:T(1,128)S(1)}, u32[]{:S(2)}, u32[]{:S(2)}) async-start(f32[32,38,1]{1,2,0:T(1,128)} %bitcast.10), calls=%async_computation.3 | async-start | bytes 32768 | tf_op jit(solution)/shard_map/all_to_all | solution.py:68
  44.3 16.8 %copy-start.18 = (f32[48]{0:T(128)}, f32[48]{0:T(128)S(1)}, u32[]{:S(2)}) copy-start(f32[48]{0:T(128)S(1)} %add_multiply_fusion) | copy-start | bytes 580
  45.1 67.2 %copy-start.5 = (f32[3072]{0:T(1024)}, f32[3072]{0:T(1024)S(1)}, u32[]{:S(2)}) copy-start(f32[3072]{0:T(1024)S(1)} %mul.272) | copy-start | bytes 36868
  51.8 1.5 copy-start.2
  55.2 0.7 copy-start.10
  55.2 0.9 copy-start.9
  55.2 0.9 copy-start.21
  75.3 7.5 %all-to-all-start.5 = ((f32[4,1,1216]{2,1,0:T(1,128)}), f32[4,1,1216]{2,1,0:T(1,128)S(1)}, u32[]{:S(2)}, u32[]{:S(2)}) async-start(f32[4,1,1216]{2,1,0:T(1,128)} %reshape.378), calls=%async_computation.5 | async-start | bytes 40960 | tf_op jit(solution)/shard_map/all_to_all | solution.py:17
  78.7 5.2 %copy-start.13 = (s32[128]{0:T(128)}, s32[128]{0:T(128)S(1)}, u32[]{:S(2)}) copy-start(s32[128]{0:T(128)S(1)} %min.18) | copy-start | bytes 1540
  78.9 5.1 %copy-start.15 = (pred[128]{0:T(512)(128)(4,1)}, pred[128]{0:T(512)(128)(4,1)S(1)}, u32[]{:S(2)}) copy-start(pred[128]{0:T(512)(128)(4,1)S(1)} %and.36) | copy-start | bytes 388
  113.6 3.2 %copy-start.19 = (f32[48]{0:T(128)S(1)}, f32[48]{0:T(128)}, u32[]{:S(2)}) copy-start(f32[48]{0:T(128)} %copy-done.18) | copy-start | bytes 580
  116.9 21.1 %copy-start.7 = (f32[38,256]{1,0:T(8,128)S(1)}, f32[38,256]{1,0:T(8,128)}, u32[]{:S(2)}) copy-start(f32[38,256]{1,0:T(8,128)} %param.17) | copy-start | bytes 116740
  184.2 3.8 %copy-start.11 = (f32[48]{0:T(128)S(1)}, f32[48]{0:T(128)}, u32[]{:S(2)}) copy-start(f32[48]{0:T(128)} %param.14) | copy-start | bytes 580
  188.0 2.2 copy-start.6
  191.6 3.3 %copy-start.1 = (f32[3072,128]{1,0:T(8,128)S(1)}, f32[3072,128]{1,0:T(8,128)}, u32[]{:S(2)}) copy-start(f32[3072,128]{1,0:T(8,128)} %get-tuple-element.12) | copy-start | bytes 4718596
  191.6 3.3 %copy-start.20 = (f32[48]{0:T(128)S(1)}, f32[48]{0:T(128)}, u32[]{:S(2)}) copy-start(f32[48]{0:T(128)} %copy-done.18) | copy-start | bytes 580
  194.9 20.6 %copy-start.8 = (f32[38,256]{1,0:T(8,128)S(1)}, f32[38,256]{1,0:T(8,128)}, u32[]{:S(2)}) copy-start(f32[38,256]{1,0:T(8,128)} %param.17) | copy-start | bytes 116740
  195.0 20.6 %copy-start.14 = (s32[128]{0:T(128)S(1)}, s32[128]{0:T(128)}, u32[]{:S(2)}) copy-start(s32[128]{0:T(128)} %copy-done.13) | copy-start | bytes 1540
  195.0 20.6 %copy-start.16 = (pred[128]{0:T(512)(128)(4,1)S(1)}, pred[128]{0:T(512)(128)(4,1)}, u32[]{:S(2)}) copy-start(pred[128]{0:T(512)(128)(4,1)} %copy-done.15) | copy-start | bytes 388
where the time goes:
time: 244 us; the launch traced here: 242 us
  blocking collectives  127 us (52%)
  matrix products  36.6 us (15%)
  starting transfers between devices  23.6 us (10%)
  waiting for transfers between devices  20.1 us (8%)
  other arithmetic  15.8 us (6%)
  local copies, waits for them, and re-layouts  11.5 us (5%)
  between operations  7.26 us (3%)
    all_to_all x9, blocking collectives, sent_to_all(): return lax.all_to_all(copies, axis, split_axis=0, concat_axis=0, tiled=True)  81.7 us
    all_to_all x2, blocking collectives, sum_by_axis(): lax.all_to_all(nearer, far, split_axis=0, concat_axis=0, tiled=True)  26 us
    all_to_all x3, blocking collectives, sum_at_owner(): lax.all_to_all(tiles, axis, split_axis=0, concat_axis=0, tiled=True)  19.8 us
    dot_general x6, matrix products, adjoint_pass(): jnp.dot(adjoint.reshape(row_count * sample_count, feature_width), weights...  16.9 us
    all_to_all x3, starting transfers between devices, sent_to_all(): return lax.all_to_all(copies, axis, split_axis=0, concat_axis=0, tiled=True)  16.9 us
    all_to_all x3, waiting for transfers between devices, sent_to_all(): return lax.all_to_all(copies, axis, split_axis=0, concat_axis=0, tiled=True)  13.9 us
    dot_general x4, matrix products, tangent_pass(): jnp.dot(tangent.reshape(row_count * sample_count, feature_width), weights...  11.2 us
    all_to_all x1, starting transfers between devices, sum_by_axis(): lax.all_to_all(nearer, far, split_axis=0, concat_axis=0, tiled=True)  6.72 us
  transfers between devices with their start and end apart: 4, of which 4 were waited for; matrix products, arithmetic and copies ran while one was open for 1% of the time, Pallas kernels for 0%

commit v1 on v0

v1 whole, which is shorter than its diff:
```python
import functools

import jax
import jax.numpy as jnp
from jax import lax
from jax.experimental import pallas as pl
from jax.experimental.pallas import tpu as pltpu
from jax.sharding import PartitionSpec as P

F = jnp.float32
B = jnp.bfloat16
MESH = pl.DeviceIdType.MESH
BOTH = ("cam", "ray")
N = 128
D = 128
SAMPLES = 48
COLORS = 3
RAYS = 64
LAYERS = 4
PARAMS = 38
COLS = 256
CG_ITERS = 2
STEP_RAYS = 32
HI = lax.Precision.HIGHEST
OFFS = (0, 40, 72, 96, 112)


def hops(d):
    return min(d, 4 - d)


OTHERS = sorted(
    (
        (dz, dc, dy, dx)
        for dz in range(4)
        for dc in range(2)
        for dy in range(4)
        for dx in range(4)
        if (dz, dc, dy, dx) != (0, 0, 0, 0)
    ),
    key=lambda o: -(hops(o[0]) + hops(o[2]) + hops(o[3])),
)


def partners():
    cam, ray = lax.axis_index("cam"), lax.axis_index("ray")
    z, c, y, x = cam // 2, cam % 2, ray // 4, ray % 4
    zs = [(z + d) % 4 * 2 for d in range(4)]
    cs = [(c + d) % 2 for d in range(2)]
    ys = [(y + d) % 4 * 4 for d in range(4)]
    xs = [(x + d) % 4 for d in range(4)]
    cams = {(dz, dc): zs[dz] + cs[dc] for dz in range(4) for dc in range(2)}
    rays = {(dy, dx): ys[dy] + xs[dx] for dy in range(4) for dx in range(4)}
    return cam * 16 + ray, [(cams[o[:2]], rays[o[2:]]) for o in OTHERS]


def dot(a, b, dims, precision=HI):
    return lax.dot_general(a, b, (dims, ((), ())), precision=precision, preferred_element_type=F)


def mlp(enc, de, w, wt, hw, quad, depth, grads, mixed):
    rows = STEP_RAYS * SAMPLES
    quad, depth = quad[None], depth[None]

    def step(t, carry):
        at = pl.ds(pl.multiple_of(t * STEP_RAYS, STEP_RAYS), STEP_RAYS)
        h = jnp.tanh(enc[at].astype(F) + de[None]).astype(B).reshape(rows, D)
        hs = [h]
        for layer in range(LAYERS):
            h = jnp.tanh(jnp.dot(h, w[layer], preferred_element_type=F)).astype(B)
            hs.append(h)
        last = h.astype(F).reshape(STEP_RAYS, SAMPLES, D)
        mixed[at] = jnp.sum(quad * last, axis=1)
        slope = ((1.0 - last * last) * quad).reshape(rows, D)
        ys = [(slope * hw[c : c + 1]).astype(B) for c in range(COLORS)]
        for layer in range(LAYERS - 1, 0, -1):
            inner = hs[layer].astype(F)
            slope = 1.0 - inner * inner
            ys = [(jnp.dot(y, wt[layer], preferred_element_type=F) * slope).astype(B) for y in ys]
        first = hs[0].astype(F).reshape(STEP_RAYS, SAMPLES, D)
        slope = (1.0 - first * first) * depth
        for c in range(COLORS):
            inner = jnp.dot(ys[c], wt[0], preferred_element_type=F)
            grads[c, at] = jnp.sum(inner.reshape(STEP_RAYS, SAMPLES, D) * slope, axis=1)
        return carry

    lax.fori_loop(0, RAYS // STEP_RAYS, step, 0)


def matvec(tiles, v):
    sub = lax.broadcasted_iota(jnp.int32, (8, N), 0)
    outs = [jnp.zeros((8, N), F) for _ in range(5)]
    for r in range(8):
        for a in range(5):
            if 8 * a + r >= PARAMS:
                continue
            own = v[a][r : r + 1]
            total = None
            for j in range(a, 5):
                at = OFFS[a] + 8 * (j - a)
                piece = tiles[r, at : at + 8]
                term = piece * v[j]
                total = term if total is None else total + term
                if j > a:
                    outs[j] = outs[j] + piece * own
            row = jnp.sum(total, axis=0, keepdims=True)
            outs[a] = outs[a] + jnp.where(sub == r, row, 0.0)
    return outs


def kernel(
    ids_in, quad_in, enc_in, targets_in, w_in, hw_in, lift_in, params_in, damping_in,
    update_out, residual_out,
    enc, owned, lift, wt, quad, id_row, ids, reply, columns, grads, mixed, tile, tiles, turned,
    local_sem, send_sem, recv_sem,
):
    me, others = partners()

    def exchange(n, source, target):
        for p in others:
            pltpu.make_async_remote_copy(
                source(p), target.at[me], send_sem.at[n], recv_sem.at[n],
                device_id=p, device_id_type=MESH,
            ).start()

    def landed(n, target):
        all_others = target.at[pl.ds(0, N - 1)]
        pltpu.make_async_copy(all_others, all_others, recv_sem.at[n]).wait()

    def sent(n, target):
        all_others = target.at[pl.ds(0, N - 1)]
        pltpu.make_async_copy(all_others, all_others, send_sem.at[n]).wait()

    barrier = pltpu.get_barrier_semaphore()
    for p in others:
        pl.semaphore_signal(barrier, inc=1, device_id=p, device_id_type=MESH)
    load = pltpu.make_async_copy(enc_in, enc, local_sem.at[0])
    load.start()

    id_row[0] = jnp.full((8, D), ids_in[0].astype(F), F)
    owned[...] = jnp.zeros_like(owned)
    owned[0:PARAMS] = params_in[...]
    owned[40 : 40 + PARAMS] = damping_in[...]
    lift[...] = jnp.zeros_like(lift)
    lift[0:PARAMS] = lift_in[...]
    for layer in range(LAYERS):
        wt[layer] = w_in[layer].T
    for s in range(SAMPLES):
        quad[s : s + 1] = jnp.full((1, D), quad_in[s], F)
    depth = (lax.broadcasted_iota(jnp.int32, (SAMPLES, D), 0).astype(F) + 1.0) / SAMPLES
    hw = hw_in[...].astype(F)
    pl.semaphore_wait(barrier, N - 1)

    exchange(0, lambda p: id_row.at[0, pl.ds(0, 1)], ids)
    ids[me] = id_row[0, 0:1]
    landed(0, ids)
    lane = lax.broadcasted_iota(jnp.int32, (N, D), 1).astype(F)
    base = (me * COLS).astype(F)
    asked = ids[...].reshape(N, D) - base
    picked = jnp.concatenate(
        [(asked == lane).astype(F), (asked == lane + 128.0).astype(F)], axis=1
    )
    reply[...] = dot(picked, owned[...], ((1,), (1,))).reshape(N, 1, D)
    exchange(1, lambda p: reply.at[p[0] * 16 + p[1]], columns)
    columns[me] = reply[me]
    landed(1, columns)
    column = jnp.sum(columns[...].reshape(N, D), axis=0, keepdims=True)
    lifted = dot(jnp.broadcast_to(column, (8, D)), lift[...], ((1,), (0,)))[0:1]
    load.wait()
    mlp(enc, depth * lifted, w_in, wt, hw, quad[...], depth, grads, mixed)

    residual = dot(hw, mixed[...], ((1,), (1,))) - targets_in[...]
    lane8 = lax.broadcasted_iota(jnp.int32, (8, D), 1)
    sub8 = lax.broadcasted_iota(jnp.int32, (8, D), 0)
    rows = dot(grads[...].reshape(COLORS * RAYS, D), lift[...], ((1,), (1,)))
    matrix = dot(rows.T[0:40], rows, ((1,), (0,)))
    right = jnp.zeros((1, D), F)
    for c in range(COLORS):
        part = rows[c * RAYS : (c + 1) * RAYS]
        right = right - dot(residual[c : c + 1], part, ((1,), (0,)))
    right = jnp.broadcast_to(right, (8, D))
    damp = pltpu.roll(jnp.broadcast_to(column, (8, D)), D - 40, axis=1)
    damp = jnp.where(lane8 == PARAMS, id_row[0], damp)
    out = jnp.zeros((8, D), F)
    for a in range(5):
        moved = matrix[8 * a : 8 * a + 8]
        if a:
            moved = pltpu.roll(moved, OFFS[a] - 8 * a, axis=1)
        inside = (lane8 >= OFFS[a]) & (lane8 < OFFS[a] + 40 - 8 * a)
        out = jnp.where(inside, moved, out)
    for value, sub, first, start in (
        [(right, m, 8 * m, 120) for m in range(5)]
        + [(damp, 5 + m, 8 * m, 120) for m in range(3)]
        + [(damp, 6, 24, 112), (damp, 7, 32, 112)]
    ):
        moved = pltpu.roll(value, start - first, axis=1)
        inside = (sub8 == sub) & (lane8 >= start) & (lane8 < start + 8)
        out = jnp.where(inside, moved, out)
    tile[0] = out
    exchange(2, lambda p: tile.at[0], tiles)
    tiles[me] = tile[0]
    landed(2, tiles)

    for r in range(8):
        turned[r] = tiles[:, r, :].T
    rhs = jnp.concatenate([turned[m, 120:128] for m in range(5)], axis=0)
    damping = jnp.concatenate(
        [turned[5, 120:128], turned[6, 120:128], turned[7, 120:128], turned[6, 112:120],
         turned[7, 112:120]], axis=0,
    )
    id_lanes = damping[PARAMS : PARAMS + 1]
    row40 = lax.broadcasted_iota(jnp.int32, (40, N), 0)
    damping = jnp.where(row40 < PARAMS, damping, 0.0)
    id_subs = tiles[:, 7, 112 + 6 : 112 + 7]
    same = id_subs == id_lanes
    earlier = lax.broadcasted_iota(jnp.int32, (N, N), 0) < lax.broadcasted_iota(jnp.int32, (N, N), 1)
    repeats = jnp.sum(jnp.where(same & earlier, 1.0, 0.0), axis=0, keepdims=True)
    once = jnp.where(repeats == 0.0, 1.0, 0.0)
    same = same.astype(F)

    def total(v):
        return jnp.sum(jnp.sum(v * once, axis=0, keepdims=True), axis=1, keepdims=True)

    def operator(v):
        product = matvec(turned, [v[8 * a : 8 * a + 8] for a in range(5)])
        return dot(jnp.concatenate(product, axis=0), same, ((1,), (0,))) + damping * v

    remainder = dot(rhs, same, ((1,), (0,)))
    direction = remainder
    norm = total(remainder * remainder)
    answer = jnp.zeros_like(remainder)
    for it in range(CG_ITERS):
        image = operator(direction)
        step = norm / total(direction * image)
        answer = answer + step * direction
        remainder = remainder - step * image
        if it + 1 < CG_ITERS:
            norm_next = total(remainder * remainder)
            direction = remainder + (norm_next / norm) * direction
            norm = norm_next
    mine = id_subs - base
    wide = lax.broadcasted_iota(jnp.int32, (N, COLS), 1).astype(F)
    place = (mine == wide).astype(F)
    update_out[...] = dot(answer * once, place, ((1,), (0,)))[0:PARAMS]
    residual_out[...] = dot(remainder * once, place, ((1,), (0,)))[0:PARAMS]
    sent(0, ids)
    sent(1, columns)
    sent(2, tiles)


def body(encodings, ray_camera, targets, weights, head_weight, quadrature, lift, cam_params, damping):
    vmem = pl.BlockSpec(memory_space=pltpu.VMEM)
    smem = pl.BlockSpec(memory_space=pltpu.SMEM)
    out = jax.ShapeDtypeStruct((PARAMS, COLS), F)
    return pl.pallas_call(
        kernel,
        out_shape=(out, out),
        in_specs=[smem, smem, pl.BlockSpec(memory_space=pl.ANY)] + [vmem] * 6,
        out_specs=(vmem, vmem),
        scratch_shapes=[
            pltpu.VMEM((RAYS, SAMPLES, D), B),
            pltpu.VMEM((D, COLS), F),
            pltpu.VMEM((D, D), F),
            pltpu.VMEM((LAYERS, D, D), B),
            pltpu.VMEM((SAMPLES, D), F),
            pltpu.VMEM((1, 8, D), F),
            pltpu.VMEM((N, 1, D), F),
            pltpu.VMEM((N, 1, D), F),
            pltpu.VMEM((N, 1, D), F),
            pltpu.VMEM((COLORS, RAYS, D), F),
            pltpu.VMEM((RAYS, D), F),
            pltpu.VMEM((1, 8, D), F),
            pltpu.VMEM((N, 8, D), F),
            pltpu.VMEM((8, D, N), F),
            pltpu.SemaphoreType.DMA((1,)),
            pltpu.SemaphoreType.DMA((3,)),
            pltpu.SemaphoreType.DMA((3,)),
        ],
        name="pose_update",
        compiler_params=pltpu.CompilerParams(
            collective_id=0, has_side_effects=True, vmem_limit_bytes=60 * 2**20
        ),
    )(ray_camera, quadrature, encodings, targets.T, weights, head_weight.T, lift, cam_params, damping)


def solution(mesh):
    in_specs = (
        P(BOTH, None, None), P(BOTH), P(BOTH, None), P(), P(), P(), P(), P(None, BOTH), P(None, BOTH),
    )
    out_specs = (P(None, BOTH), P(None, BOTH))
    return jax.shard_map(body, mesh=mesh, in_specs=in_specs, out_specs=out_specs, check_vma=False)
```

time: 244 us -> 42.3 us (0.17)
  blocking collectives: 127 us -> 0 us
  Pallas kernels: 0 us -> 39.4 us
  matrix products: 36.6 us -> 0 us
  starting transfers between devices: 23.6 us -> 0 us
  waiting for transfers between devices: 20.1 us -> 0 us
  other arithmetic: 15.8 us -> 0 us
  local copies, waits for them, and re-layouts: 11.5 us -> 2.03 us
  between operations: 7.26 us -> 0.65 us
    all_to_all x14 -> x0, blocking collectives: 127 us -> none  [the longest x9 81.7 us: sent_to_all(): return lax.all_to_all(copies, axis, split_axis=0, concat_axis=0, tiled=True)]
    pallas_call x0 -> x1, Pallas kernels: none -> 39.4 us  [body(): pl.pallas_call(kernel, out_shape=(out, out), in_specs=[smem, smem, pl.Blo...]
    dot_general x29 -> x0, matrix products: 36.6 us -> none  [the longest x6 16.9 us: adjoint_pass(): jnp.dot(adjoint.reshape(row_count * sample_count, feature_width), weights...]
    all_to_all x4 -> x0, starting transfers between devices: 23.6 us -> none  [the longest x3 16.9 us: sent_to_all(): return lax.all_to_all(copies, axis, split_axis=0, concat_axis=0, tiled=True)]
    all_to_all x4 -> x0, waiting for transfers between devices: 20.1 us -> none  [the longest x3 13.9 us: sent_to_all(): return lax.all_to_all(copies, axis, split_axis=0, concat_axis=0, tiled=True)]
    all_to_all x7 -> x0, other arithmetic: 5.04 us -> none  [the longest x4 2.85 us: sent_to_all(): return lax.all_to_all(copies, axis, split_axis=0, concat_axis=0, tiled=True)]
    convert_element_type x4 -> x0, other arithmetic: 4.42 us -> none  [the longest x3 4.08 us: adjoint_pass(): (slope * quadrature[None, :, None] * cotangent[:, None, :]).astype(jnp.bf...]
    concatenate x2 -> x0, other arithmetic: 2.76 us -> none  [packed_total(): line, at, outs = (jnp.concatenate([a.reshape(-1) for a in arrays]), 0, [])]
  transfers between devices with their start and end apart: 4 -> 0, of which waited for: 4 -> 0; matrix products, arithmetic and copies ran while one was open for 1% -> 0% of each run, Pallas kernels for 0% -> 0%
where the time goes in v1:
time: 42.3 us; the launch traced here: 42.1 us
  Pallas kernels  39.4 us (93%)
  local copies, waits for them, and re-layouts  2.03 us (5%)
  between operations  0.65 us (2%)
    pallas_call x1, Pallas kernels, body(): pl.pallas_call(kernel, out_shape=(out, out), in_specs=[smem, smem, pl.Blo...  39.4 us
    unnamed x4, local copies, waits for them, and re-layouts  2.03 us

profile of v1, /device:TPU:1, one launch (start us, length us, event | category | flops | bytes accessed | tf_op | source)
XLA Modules:
  0.0 42.1 jit_solution(1509993157568125576)
XLA Ops:
  0.6 39.4 %pose_update.1 = (f32[38,256]{1,0:T(8,128)}, f32[38,256]{1,0:T(8,128)}) custom-call(s32[64]{0:T(128)} %ids_in.1, f32[48]{0:T(128)} %quad_in.1, bf16[64,48,128]{2,1,0:T(8,128)(2,1)} %enc_in.1, f32[3,64]{1,0:T(4,128)} %bitcast.2, bf16[4,128,128]{2,1,0:T(8,128)(2,1)} %w_in.1, bf16[3,128]{1,0:T(4,128)(2,1)} %bitcast.3, f32[38,128]{1,0:T(8,128)} %lift_in.1, ...), custom_call_target="tpu_custom_call" | custom-call | tf_op jit(solution)/shard_map/pose_update/pallas_call | solution.py:255
  40.1 0.0 copy-start
  40.1 1.4 %copy.13 = f32[38,256]{1,0:T(8,128)} copy(f32[38,256]{1,0:T(8,128)} %get-tuple-element.4) | data formatting | bytes 77824
  41.5 0.0 copy-done
  41.5 0.6 %copy.14 = f32[38,256]{1,0:T(8,128)} copy(f32[38,256]{1,0:T(8,128)S(1)} %copy-done) | data formatting | bytes 77824
Async XLA Ops:
  40.1 1.4 %copy-start = (f32[38,256]{1,0:T(8,128)S(1)}, f32[38,256]{1,0:T(8,128)}, u32[]{:S(2)}) copy-start(f32[38,256]{1,0:T(8,128)} %get-tuple-element.5) | copy-start | bytes 116740

commit v2 on v1

v2 whole, which is shorter than its diff:
```python
import functools

import jax
import jax.numpy as jnp
from jax import lax
from jax.experimental import pallas as pl
from jax.experimental.pallas import tpu as pltpu
from jax.sharding import PartitionSpec as P

F = jnp.float32
B = jnp.bfloat16
MESH = pl.DeviceIdType.MESH
BOTH = ("cam", "ray")
N = 128
D = 128
SAMPLES = 48
COLORS = 3
RAYS = 64
LAYERS = 4
PARAMS = 38
COLS = 256
CG_ITERS = 2
STEP_RAYS = 32
HI = lax.Precision.HIGHEST
OFFS = (0, 40, 72, 96, 112)


def far(o):
    return sum(min(d, 4 - d) for d in (o[0], o[2], o[3]))


OTHERS = sorted(
    (
        (dz, dc, dy, dx)
        for dz in range(4)
        for dc in range(2)
        for dy in range(4)
        for dx in range(4)
        if (dz, dc, dy, dx) != (0, 0, 0, 0)
    ),
    key=lambda o: -far(o),
)
PLANE = [o for o in OTHERS if o[3] == 0]
LINE = [o for o in OTHERS if o[:3] == (0, 0, 0)]
SAME = [o for o in OTHERS if o[1] == 0]
PAIR = (0, 1, 0, 0)
ASKERS = len(PLANE) + 1
HALF = len(SAME) + 1
GROUPS = [[i for i, o in enumerate(SAME) if far(o) in hops] for hops in ((1, 2), (3,), (4, 5, 6))]


def device(o):
    cam, ray = lax.axis_index("cam"), lax.axis_index("ray")
    z, c, y, x = cam // 2, cam % 2, ray // 4, ray % 4
    return (z + o[0]) % 4 * 2 + (c + o[1]) % 2, (y + o[2]) % 4 * 4 + (x + o[3]) % 4


def opposite(o):
    return (-o[0]) % 4, (-o[1]) % 2, (-o[2]) % 4, (-o[3]) % 4


def dot(a, b, dims, precision=HI):
    return lax.dot_general(a, b, (dims, ((), ())), precision=precision, preferred_element_type=F)


def dot_ones(a, b, dims):
    high = a.astype(B)
    rest = a - high.astype(F)
    middle = rest.astype(B)
    low = (rest - middle.astype(F)).astype(B)
    n = a.shape[0]
    out = dot(jnp.concatenate([high, middle, low], axis=0), b, dims, None)
    return out[0:n] + out[n : 2 * n] + out[2 * n : 3 * n]


def mlp(enc, de, w, wt, hw, quad, depth, grads, mixed):
    rows = STEP_RAYS * SAMPLES
    quad, depth = quad[None], depth[None]

    def step(t, carry):
        at = pl.ds(pl.multiple_of(t * STEP_RAYS, STEP_RAYS), STEP_RAYS)
        h = jnp.tanh(enc[at].astype(F) + de[None]).astype(B).reshape(rows, D)
        hs = [h]
        for layer in range(LAYERS):
            h = jnp.tanh(jnp.dot(h, w[layer], preferred_element_type=F)).astype(B)
            hs.append(h)
        last = h.astype(F).reshape(STEP_RAYS, SAMPLES, D)
        mixed[at] = jnp.sum(quad * last, axis=1)
        slope = ((1.0 - last * last) * quad).reshape(rows, D)
        ys = [(slope * hw[c : c + 1]).astype(B) for c in range(COLORS)]
        for layer in range(LAYERS - 1, 0, -1):
            inner = hs[layer].astype(F)
            slope = 1.0 - inner * inner
            ys = [(jnp.dot(y, wt[layer], preferred_element_type=F) * slope).astype(B) for y in ys]
        first = hs[0].astype(F).reshape(STEP_RAYS, SAMPLES, D)
        slope = (1.0 - first * first) * depth
        for c in range(COLORS):
            inner = jnp.dot(ys[c], wt[0], preferred_element_type=F)
            grads[c, at] = jnp.sum(inner.reshape(STEP_RAYS, SAMPLES, D) * slope, axis=1)
        return carry

    lax.fori_loop(0, RAYS // STEP_RAYS, step, 0)


def matvec(turned, v):
    sub = lax.broadcasted_iota(jnp.int32, (8, N), 0)
    outs = [jnp.zeros((8, N), F) for _ in range(5)]
    for r in range(8):
        for a in range(5):
            if 8 * a + r >= PARAMS:
                continue
            own = v[a][r : r + 1]
            total = None
            for j in range(a, 5):
                at = OFFS[a] + 8 * (j - a)
                piece = turned[r, at : at + 8]
                term = piece * v[j]
                total = term if total is None else total + term
                if j > a:
                    outs[j] = outs[j] + piece * own
            row = jnp.sum(total, axis=0, keepdims=True)
            outs[a] = outs[a] + jnp.where(sub == r, row, 0.0)
    return outs


def kernel(
    quad_in, ids_in, enc_in, targets_in, w_in, hw_in, lift_in, params_in, damping_in,
    result_out,
    enc, targets, w, hw_b, lift_b, wt, lift, quad, ids, owned, owned_damping,
    reply, reply_damping, columns, columns_damping, grads, mixed, tiles, turned,
    load_sem, send_sem, recv_sem, group_sem,
):
    def send(source, target, n, o, recv=None):
        pltpu.make_async_remote_copy(
            source, target, send_sem.at[n], recv_sem.at[n] if recv is None else recv,
            device_id=device(o), device_id_type=MESH,
        ).start()

    def wait(ref, sem):
        pltpu.make_async_copy(ref, ref, sem).wait()

    barrier = pltpu.get_barrier_semaphore()
    for o in PLANE + LINE:
        pl.semaphore_signal(barrier, inc=1, device_id=device(o), device_id_type=MESH)
    loads = [
        pltpu.make_async_copy(source, target, load_sem.at[i])
        for i, (source, target) in enumerate(
            [
                (ids_in, ids.at[ASKERS - 1]),
                (params_in, owned.at[0]),
                (damping_in, owned_damping.at[0]),
                (lift_in, lift_b),
                (w_in, w),
                (hw_in, hw_b),
                (targets_in, targets),
                (enc_in, enc),
            ]
        )
    ]
    for load in loads:
        load.start()

    reply[...] = jnp.zeros_like(reply)
    reply_damping[...] = jnp.zeros_like(reply_damping)
    lift[...] = jnp.zeros_like(lift)
    for s in range(SAMPLES):
        quad[s : s + 1] = jnp.full((1, D), quad_in[s], F)
    depth = (lax.broadcasted_iota(jnp.int32, (SAMPLES, D), 0).astype(F) + 1.0) / SAMPLES
    loads[0].wait()
    loads[1].wait()
    pl.semaphore_wait(barrier, len(PLANE) + len(LINE))

    for o in LINE:
        send(owned.at[0], owned.at[o[3]], 1, o)
    for i, o in enumerate(PLANE):
        send(ids.at[ASKERS - 1], ids.at[i], 0, o)
    loads[2].wait()
    for o in LINE:
        send(owned_damping.at[0], owned_damping.at[o[3]], 2, o)
    for load in loads[3:7]:
        load.wait()
    lift[0:PARAMS] = lift_b[...]
    for layer in range(LAYERS):
        wt[layer] = w[layer].T
    hw = hw_b[...].astype(F)
    wait(ids.at[pl.ds(0, ASKERS - 1)], recv_sem.at[0])

    asked = ids[...].reshape(ASKERS, RAYS).astype(F)
    here = lax.broadcasted_iota(jnp.int32, (ASKERS, RAYS), 0) == lax.broadcasted_iota(
        jnp.int32, (ASKERS, RAYS), 1
    )
    asked = jnp.sum(jnp.where(here, asked, 0.0), axis=0, keepdims=True)
    count = lax.broadcasted_iota(jnp.int32, (COLS, RAYS), 0).astype(F)
    picked = []
    for t in range(4):
        cam, ray = device((0, 0, 0, (4 - t) % 4))
        first = ((cam * 16 + ray) * COLS).astype(F)
        picked.append((asked - first == count).astype(B))
    picked = jnp.concatenate(picked, axis=0)

    def answer(held, rows, landing, n):
        wide = jnp.concatenate([held[t] for t in range(4)], axis=1)
        wide = jnp.concatenate([wide, jnp.zeros((2, 4 * COLS), F)], axis=0)
        got = dot_ones(wide, picked, ((1,), (0,)))
        rows[:, 0, 0:40] = got.T[0:ASKERS]
        for i, o in enumerate(PLANE):
            send(rows.at[i], landing.at[i], n, opposite(o))
        landing[ASKERS - 1] = rows[ASKERS - 1]

    wait(owned.at[pl.ds(1, 3)], recv_sem.at[1])
    answer(owned, reply, columns, 3)
    wait(owned_damping.at[pl.ds(1, 3)], recv_sem.at[2])
    answer(owned_damping, reply_damping, columns_damping, 4)
    wait(columns.at[pl.ds(0, ASKERS - 1)], recv_sem.at[3])
    column = jnp.sum(columns[...].reshape(ASKERS, D), axis=0, keepdims=True)
    lifted = dot(jnp.broadcast_to(column, (8, D)), lift[...], ((1,), (0,)))[0:1]
    loads[7].wait()
    mlp(enc, depth * lifted, w, wt, hw, quad[...], depth, grads, mixed)

    wait(columns_damping.at[pl.ds(0, ASKERS - 1)], recv_sem.at[4])
    damp = jnp.sum(columns_damping[...].reshape(ASKERS, D), axis=0, keepdims=True)
    residual = dot(hw, mixed[...], ((1,), (1,))) - targets[...]
    lane8 = lax.broadcasted_iota(jnp.int32, (8, D), 1)
    sub8 = lax.broadcasted_iota(jnp.int32, (8, D), 0)
    rows = dot(grads[...].reshape(COLORS * RAYS, D), lift[...], ((1,), (1,)))
    matrix = dot(rows.T[0:40], rows, ((1,), (0,)))
    right = jnp.zeros((1, D), F)
    for c in range(COLORS):
        part = rows[c * RAYS : (c + 1) * RAYS]
        right = right - dot(residual[c : c + 1], part, ((1,), (0,)))
    right = jnp.broadcast_to(right, (8, D))
    camera = ids[ASKERS - 1][:, 0:1].astype(F)
    damp = jnp.where(lane8 == PARAMS, camera, jnp.broadcast_to(damp, (8, D)))
    out = jnp.zeros((8, D), F)
    for a in range(5):
        moved = matrix[8 * a : 8 * a + 8]
        if a:
            moved = pltpu.roll(moved, OFFS[a] - 8 * a, axis=1)
        inside = (lane8 >= OFFS[a]) & (lane8 < OFFS[a] + 40 - 8 * a)
        out = jnp.where(inside, moved, out)
    for value, sub, first, start in (
        [(right, m, 8 * m, 120) for m in range(5)]
        + [(damp, 5 + m, 8 * m, 120) for m in range(3)]
        + [(damp, 6, 24, 112), (damp, 7, 32, 112)]
    ):
        moved = pltpu.roll(value, start - first, axis=1)
        inside = (sub8 == sub) & (lane8 >= start) & (lane8 < start + 8)
        out = jnp.where(inside, moved, out)
    tiles[HALF - 1] = out
    for g in (2, 1, 0):
        for i in GROUPS[g]:
            send(tiles.at[HALF - 1], tiles.at[i], 5, SAME[i], group_sem.at[g])
    for g in range(3):
        at, n = GROUPS[g][0], len(GROUPS[g])
        wait(tiles.at[pl.ds(at, n)], group_sem.at[g])
        n += g == 0
        send(tiles.at[pl.ds(at, n)], tiles.at[pl.ds(HALF + at, n)], 6, PAIR)
    wait(tiles.at[pl.ds(HALF, HALF)], recv_sem.at[6])

    for r in range(8):
        turned[r] = tiles[:, r, :].T
    rhs = jnp.concatenate([turned[m, 120:128] for m in range(5)], axis=0)
    damping = jnp.concatenate(
        [turned[5, 120:128], turned[6, 120:128], turned[7, 120:128], turned[6, 112:120],
         turned[7, 112:120]], axis=0,
    )
    id_lanes = damping[PARAMS : PARAMS + 1]
    row40 = lax.broadcasted_iota(jnp.int32, (40, N), 0)
    damping = jnp.where(row40 < PARAMS, damping, 0.0)
    id_subs = tiles[:, 7, 112 + 6 : 112 + 7]
    same = id_subs == id_lanes
    earlier = lax.broadcasted_iota(jnp.int32, (N, N), 0) < lax.broadcasted_iota(jnp.int32, (N, N), 1)
    repeats = jnp.sum(jnp.where(same & earlier, 1.0, 0.0), axis=0, keepdims=True)
    once = jnp.where(repeats == 0.0, 1.0, 0.0)
    same = same.astype(B)

    def total(v):
        return jnp.sum(jnp.sum(v * once, axis=0, keepdims=True), axis=1, keepdims=True)

    def operator(v):
        product = matvec(turned, [v[8 * a : 8 * a + 8] for a in range(5)])
        return dot_ones(jnp.concatenate(product, axis=0), same, ((1,), (0,))) + damping * v

    remainder = dot_ones(rhs, same, ((1,), (0,)))
    direction = remainder
    norm = total(remainder * remainder)
    answered = jnp.zeros_like(remainder)
    for it in range(CG_ITERS):
        image = operator(direction)
        step = norm / total(direction * image)
        answered = answered + step * direction
        remainder = remainder - step * image
        if it + 1 < CG_ITERS:
            norm_next = total(remainder * remainder)
            direction = remainder + (norm_next / norm) * direction
            norm = norm_next
    result_out[0:40] = answered * once
    result_out[40:80] = remainder * once
    result_out[80:88] = jnp.broadcast_to(id_lanes, (8, N))
    wait(ids.at[pl.ds(0, ASKERS - 1)], send_sem.at[0])
    wait(owned.at[pl.ds(1, 3)], send_sem.at[1])
    wait(owned_damping.at[pl.ds(1, 3)], send_sem.at[2])
    wait(columns.at[pl.ds(0, ASKERS - 1)], send_sem.at[3])
    wait(columns_damping.at[pl.ds(0, ASKERS - 1)], send_sem.at[4])
    wait(tiles.at[pl.ds(0, HALF - 1)], send_sem.at[5])
    wait(tiles.at[pl.ds(HALF, HALF)], send_sem.at[6])


def place(result, update_out, residual_out):
    first = ((lax.axis_index("cam") * 16 + lax.axis_index("ray")) * COLS).astype(F)
    count = lax.broadcasted_iota(jnp.int32, (COLS, N), 0).astype(F)
    where = (result[80:81] - first == count).astype(B)
    out = dot_ones(result[0:80], where, ((1,), (1,)))
    update_out[...] = out[0:PARAMS]
    residual_out[...] = out[40 : 40 + PARAMS]


def body(encodings, ray_camera, targets, weights, head_weight, quadrature, lift, cam_params, damping):
    vmem = pl.BlockSpec(memory_space=pltpu.VMEM)
    smem = pl.BlockSpec(memory_space=pltpu.SMEM)
    hbm = pl.BlockSpec(memory_space=pl.ANY)
    result = pl.pallas_call(
        kernel,
        out_shape=jax.ShapeDtypeStruct((88, N), F),
        in_specs=[smem] + [hbm] * 8,
        out_specs=vmem,
        scratch_shapes=[
            pltpu.VMEM((RAYS, SAMPLES, D), B),
            pltpu.VMEM((COLORS, RAYS), F),
            pltpu.VMEM((LAYERS, D, D), B),
            pltpu.VMEM((COLORS, D), B),
            pltpu.VMEM((PARAMS, D), F),
            pltpu.VMEM((LAYERS, D, D), B),
            pltpu.VMEM((D, D), F),
            pltpu.VMEM((SAMPLES, D), F),
            pltpu.VMEM((ASKERS, 1, RAYS), jnp.int32),
            pltpu.VMEM((4, PARAMS, COLS), F),
            pltpu.VMEM((4, PARAMS, COLS), F),
            pltpu.VMEM((ASKERS, 1, D), F),
            pltpu.VMEM((ASKERS, 1, D), F),
            pltpu.VMEM((ASKERS, 1, D), F),
            pltpu.VMEM((ASKERS, 1, D), F),
            pltpu.VMEM((COLORS, RAYS, D), F),
            pltpu.VMEM((RAYS, D), F),
            pltpu.VMEM((N, 8, D), F),
            pltpu.VMEM((8, D, N), F),
            pltpu.SemaphoreType.DMA((8,)),
            pltpu.SemaphoreType.DMA((7,)),
            pltpu.SemaphoreType.DMA((7,)),
            pltpu.SemaphoreType.DMA((3,)),
        ],
        name="pose_solve",
        compiler_params=pltpu.CompilerParams(
            collective_id=0, has_side_effects=True, vmem_limit_bytes=60 * 2**20
        ),
    )(
        quadrature, ray_camera.reshape(1, RAYS), encodings, targets.T, weights, head_weight.T, lift,
        cam_params, damping,
    )
    out = jax.ShapeDtypeStruct((PARAMS, COLS), F)
    return pl.pallas_call(
        place, out_shape=(out, out), in_specs=[vmem], out_specs=(vmem, vmem), name="pose_place"
    )(result)


def solution(mesh):
    in_specs = (
        P(BOTH, None, None), P(BOTH), P(BOTH, None), P(), P(), P(), P(), P(None, BOTH), P(None, BOTH),
    )
    out_specs = (P(None, BOTH), P(None, BOTH))
    return jax.shard_map(body, mesh=mesh, in_specs=in_specs, out_specs=out_specs, check_vma=False)
```

time: 42.3 us -> 37.2 us (0.88)
  Pallas kernels: 39.4 us -> 36.4 us
  local copies, waits for them, and re-layouts: 2.03 us -> 0 us
    pallas_call x1 -> x2, Pallas kernels: 39.4 us -> 36.4 us  [the longest x1 34.7 us: body(): pl.pallas_call(kernel, out_shape=jax.ShapeDtypeStruct((88, N), F), in_spe...]
    unnamed x4 -> x0, local copies, waits for them, and re-layouts: 2.03 us -> none
where the time goes in v2:
time: 37.2 us; the launch traced here: 37 us
  Pallas kernels  36.4 us (98%)
  between operations  0.64 us (2%)
    pallas_call x1, Pallas kernels, body(): pl.pallas_call(kernel, out_shape=jax.ShapeDtypeStruct((88, N), F), in_spe...  34.7 us
    pallas_call x1, Pallas kernels, body(): pl.pallas_call(place, out_shape=(out, out), in_specs=[vmem], out_specs=(v...  1.63 us

profile of v2, /device:TPU:1, one launch (start us, length us, event | category | flops | bytes accessed | tf_op | source)
XLA Modules:
  0.0 37.0 jit_solution(6219909321342116327)
XLA Ops:
  0.6 34.7 %pose_solve.1.result = f32[88,128]{1,0:T(8,128)} custom-call(f32[48]{0:T(128)} %quad_in.1, s32[1,64]{1,0:T(1,128)} %bitcast.5, bf16[64,48,128]{2,1,0:T(8,128)(2,1)} %enc_in.1, f32[3,64]{1,0:T(4,128)} %bitcast.3, bf16[4,128,128]{2,1,0:T(8,128)(2,1)} %w_in.1, bf16[3,128]{1,0:T(4,128)(2,1)} %bitcast.4, f32[38,128]{1,0:T(8,128)} %lift_in.1, ...), custom_call_target="tpu_custom_call" | custom-call | tf_op jit(solution)/shard_map/pose_solve/pallas_call | solution.py:322
  35.4 1.6 %pose_place.1 = (f32[38,256]{1,0:T(8,128)}, f32[38,256]{1,0:T(8,128)}) custom-call(f32[88,128]{1,0:T(8,128)} %pose_solve.1.result), custom_call_target="tpu_custom_call" | custom-call | tf_op jit(solution)/shard_map/pose_place/pallas_call | solution.py:361

commit v3 on v2

--- a/solution.py
+++ b/solution.py
@@ -20,7 +20,7 @@
 PARAMS = 38
 COLS = 256
 CG_ITERS = 2
-STEP_RAYS = 32
+STEP_RAYS = 64
 HI = lax.Precision.HIGHEST
 OFFS = (0, 40, 72, 96, 112)
 
@@ -40,11 +40,16 @@
     ),
     key=lambda o: -far(o),
 )
-PLANE = [o for o in OTHERS if o[3] == 0]
-LINE = [o for o in OTHERS if o[:3] == (0, 0, 0)]
+ROW = [(dc, dy) for dc, dy in ((0, 2), (1, 2), (0, 1), (0, 3), (1, 1), (1, 3), (1, 0), (0, 0))]
+PLANE = [(dz, dc, dy, 0) for dz in range(4) for dc, dy in ROW]
+OWN = len(ROW) - 1
+ROWS = [(0, dc, dy, 0) for dc, dy in ROW[:OWN]]
+COLUMN = [(dz, 0, 0, 0) for dz in (2, 1, 3)]
+LINE = [(0, 0, 0, dx) for dx in (2, 1, 3)]
 SAME = [o for o in OTHERS if o[1] == 0]
 PAIR = (0, 1, 0, 0)
-ASKERS = len(PLANE) + 1
+ANSWERED = sorted((i for i in range(len(PLANE)) if i != OWN), key=lambda i: -far(PLANE[i]))
+ASKERS = len(PLANE)
 HALF = len(SAME) + 1
 GROUPS = [[i for i, o in enumerate(SAME) if far(o) in hops] for hops in ((1, 2), (3,), (4, 5, 6))]
 
@@ -63,14 +68,22 @@
     return lax.dot_general(a, b, (dims, ((), ())), precision=precision, preferred_element_type=F)
 
 
-def dot_ones(a, b, dims):
+def three_terms(a):
     high = a.astype(B)
     rest = a - high.astype(F)
     middle = rest.astype(B)
     low = (rest - middle.astype(F)).astype(B)
-    n = a.shape[0]
-    out = dot(jnp.concatenate([high, middle, low], axis=0), b, dims, None)
+    return jnp.concatenate([high, middle, low], axis=0)
+
+
+def dot_terms(terms, b, dims):
+    n = terms.shape[0] // 3
+    out = dot(terms, b, dims, None)
     return out[0:n] + out[n : 2 * n] + out[2 * n : 3 * n]
+
+
+def dot_ones(a, b, dims):
+    return dot_terms(three_terms(a), b, dims)
 
 
 def mlp(enc, de, w, wt, hw, quad, depth, grads, mixed):
@@ -126,7 +139,7 @@
 def kernel(
     quad_in, ids_in, enc_in, targets_in, w_in, hw_in, lift_in, params_in, damping_in,
     result_out,
-    enc, targets, w, hw_b, lift_b, wt, lift, quad, ids, owned, owned_damping,
+    enc, targets, w, hw_b, lift_b, quad_b, wt, lift, quad, ids, owned, owned_damping,
     reply, reply_damping, columns, columns_damping, grads, mixed, tiles, turned,
     load_sem, send_sem, recv_sem, group_sem,
 ):
@@ -140,19 +153,20 @@
         pltpu.make_async_copy(ref, ref, sem).wait()
 
     barrier = pltpu.get_barrier_semaphore()
-    for o in PLANE + LINE:
+    for o in ROWS + COLUMN + LINE:
         pl.semaphore_signal(barrier, inc=1, device_id=device(o), device_id_type=MESH)
     loads = [
         pltpu.make_async_copy(source, target, load_sem.at[i])
         for i, (source, target) in enumerate(
             [
-                (ids_in, ids.at[ASKERS - 1]),
+                (ids_in, ids.at[OWN]),
                 (params_in, owned.at[0]),
                 (damping_in, owned_damping.at[0]),
                 (lift_in, lift_b),
                 (w_in, w),
                 (hw_in, hw_b),
                 (targets_in, targets),
+                (quad_in, quad_b),
                 (enc_in, enc),
             ]
         )
@@ -163,27 +177,37 @@
     reply[...] = jnp.zeros_like(reply)
     reply_damping[...] = jnp.zeros_like(reply_damping)
     lift[...] = jnp.zeros_like(lift)
-    for s in range(SAMPLES):
-        quad[s : s + 1] = jnp.full((1, D), quad_in[s], F)
     depth = (lax.broadcasted_iota(jnp.int32, (SAMPLES, D), 0).astype(F) + 1.0) / SAMPLES
     loads[0].wait()
     loads[1].wait()
-    pl.semaphore_wait(barrier, len(PLANE) + len(LINE))
-
+    pl.semaphore_wait(barrier, len(ROWS) + len(COLUMN) + len(LINE))
+
+    for i, o in enumerate(ROWS):
+        send(ids.at[OWN], ids.at[i], 0, o)
     for o in LINE:
         send(owned.at[0], owned.at[o[3]], 1, o)
-    for i, o in enumerate(PLANE):
-        send(ids.at[ASKERS - 1], ids.at[i], 0, o)
     loads[2].wait()
     for o in LINE:
         send(owned_damping.at[0], owned_damping.at[o[3]], 2, o)
-    for load in loads[3:7]:
+    for load in loads[3:8]:
         load.wait()
     lift[0:PARAMS] = lift_b[...]
+    quad[...] = jnp.broadcast_to(quad_b[...], (D, SAMPLES)).T
+    hw = hw_b[...].astype(F)
+    wait(ids.at[pl.ds(0, OWN)], recv_sem.at[0])
+    row = ids.at[pl.ds(0, OWN + 1)]
+    for o in COLUMN:
+        send(row, ids.at[pl.ds(o[0] * (OWN + 1), OWN + 1)], 7, o)
     for layer in range(LAYERS):
         wt[layer] = w[layer].T
-    hw = hw_b[...].astype(F)
-    wait(ids.at[pl.ds(0, ASKERS - 1)], recv_sem.at[0])
+
+    def terms_of(held):
+        wide = jnp.concatenate([held[t] for t in range(4)], axis=1)
+        return three_terms(jnp.concatenate([wide, jnp.zeros((2, 4 * COLS), F)], axis=0))
+
+    wait(owned.at[pl.ds(1, 3)], recv_sem.at[1])
+    terms = terms_of(owned)
+    wait(ids.at[pl.ds(OWN + 1, 3 * (OWN + 1))], recv_sem.at[7])
 
     asked = ids[...].reshape(ASKERS, RAYS).astype(F)
     here = lax.broadcasted_iota(jnp.int32, (ASKERS, RAYS), 0) == lax.broadcasted_iota(
@@ -198,23 +222,20 @@
         picked.append((asked - first == count).astype(B))
     picked = jnp.concatenate(picked, axis=0)
 
-    def answer(held, rows, landing, n):
-        wide = jnp.concatenate([held[t] for t in range(4)], axis=1)
-        wide = jnp.concatenate([wide, jnp.zeros((2, 4 * COLS), F)], axis=0)
-        got = dot_ones(wide, picked, ((1,), (0,)))
+    def answer(terms, rows, landing, n):
+        got = dot_terms(terms, picked, ((1,), (0,)))
         rows[:, 0, 0:40] = got.T[0:ASKERS]
-        for i, o in enumerate(PLANE):
-            send(rows.at[i], landing.at[i], n, opposite(o))
-        landing[ASKERS - 1] = rows[ASKERS - 1]
-
-    wait(owned.at[pl.ds(1, 3)], recv_sem.at[1])
-    answer(owned, reply, columns, 3)
+        for i in ANSWERED:
+            send(rows.at[i], landing.at[i], n, opposite(PLANE[i]))
+        landing[OWN] = rows[OWN]
+
+    answer(terms, reply, columns, 3)
     wait(owned_damping.at[pl.ds(1, 3)], recv_sem.at[2])
-    answer(owned_damping, reply_damping, columns_damping, 4)
+    answer(terms_of(owned_damping), reply_damping, columns_damping, 4)
     wait(columns.at[pl.ds(0, ASKERS - 1)], recv_sem.at[3])
     column = jnp.sum(columns[...].reshape(ASKERS, D), axis=0, keepdims=True)
     lifted = dot(jnp.broadcast_to(column, (8, D)), lift[...], ((1,), (0,)))[0:1]
-    loads[7].wait()
+    loads[8].wait()
     mlp(enc, depth * lifted, w, wt, hw, quad[...], depth, grads, mixed)
 
     wait(columns_damping.at[pl.ds(0, ASKERS - 1)], recv_sem.at[4])
@@ -229,7 +250,7 @@
         part = rows[c * RAYS : (c + 1) * RAYS]
         right = right - dot(residual[c : c + 1], part, ((1,), (0,)))
     right = jnp.broadcast_to(right, (8, D))
-    camera = ids[ASKERS - 1][:, 0:1].astype(F)
+    camera = ids[OWN][:, 0:1].astype(F)
     damp = jnp.where(lane8 == PARAMS, camera, jnp.broadcast_to(damp, (8, D)))
     out = jnp.zeros((8, D), F)
     for a in range(5):
@@ -297,7 +318,8 @@
     result_out[0:40] = answered * once
     result_out[40:80] = remainder * once
     result_out[80:88] = jnp.broadcast_to(id_lanes, (8, N))
-    wait(ids.at[pl.ds(0, ASKERS - 1)], send_sem.at[0])
+    wait(ids.at[pl.ds(0, OWN)], send_sem.at[0])
+    wait(ids.at[pl.ds(OWN + 1, 3 * (OWN + 1))], send_sem.at[7])
     wait(owned.at[pl.ds(1, 3)], send_sem.at[1])
     wait(owned_damping.at[pl.ds(1, 3)], send_sem.at[2])
     wait(columns.at[pl.ds(0, ASKERS - 1)], send_sem.at[3])
@@ -317,12 +339,11 @@
 
 def body(encodings, ray_camera, targets, weights, head_weight, quadrature, lift, cam_params, damping):
     vmem = pl.BlockSpec(memory_space=pltpu.VMEM)
-    smem = pl.BlockSpec(memory_space=pltpu.SMEM)
     hbm = pl.BlockSpec(memory_space=pl.ANY)
     result = pl.pallas_call(
         kernel,
         out_shape=jax.ShapeDtypeStruct((88, N), F),
-        in_specs=[smem] + [hbm] * 8,
+        in_specs=[hbm] * 9,
         out_specs=vmem,
         scratch_shapes=[
             pltpu.VMEM((RAYS, SAMPLES, D), B),
@@ -330,6 +351,7 @@
             pltpu.VMEM((LAYERS, D, D), B),
             pltpu.VMEM((COLORS, D), B),
             pltpu.VMEM((PARAMS, D), F),
+            pltpu.VMEM((1, SAMPLES), F),
             pltpu.VMEM((LAYERS, D, D), B),
             pltpu.VMEM((D, D), F),
             pltpu.VMEM((SAMPLES, D), F),
@@ -344,9 +366,9 @@
             pltpu.VMEM((RAYS, D), F),
             pltpu.VMEM((N, 8, D), F),
             pltpu.VMEM((8, D, N), F),
+            pltpu.SemaphoreType.DMA((9,)),
             pltpu.SemaphoreType.DMA((8,)),
-            pltpu.SemaphoreType.DMA((7,)),
-            pltpu.SemaphoreType.DMA((7,)),
+            pltpu.SemaphoreType.DMA((8,)),
             pltpu.SemaphoreType.DMA((3,)),
         ],
         name="pose_solve",
@@ -354,7 +376,7 @@
             collective_id=0, has_side_effects=True, vmem_limit_bytes=60 * 2**20
         ),
     )(
-        quadrature, ray_camera.reshape(1, RAYS), encodings, targets.T, weights, head_weight.T, lift,
+        quadrature.reshape(1, SAMPLES), ray_camera.reshape(1, RAYS), encodings, targets.T, weights, head_weight.T, lift,
         cam_params, damping,
     )
     out = jax.ShapeDtypeStruct((PARAMS, COLS), F)

time: 37.2 us -> 37 us (level)
  no operation moved by 1% of the time
where the time goes in v3:
time: 37 us; the launch traced here: 36.9 us
  Pallas kernels  36.2 us (98%)
  between operations  0.64 us (2%)
    pallas_call x1, Pallas kernels, body(): pl.pallas_call(kernel, out_shape=jax.ShapeDtypeStruct((88, N), F), in_spe...  34.6 us
    pallas_call x1, Pallas kernels, body(): pl.pallas_call(place, out_shape=(out, out), in_specs=[vmem], out_specs=(v...  1.63 us

profile of v3, /device:TPU:1, one launch (start us, length us, event | category | flops | bytes accessed | tf_op | source)
XLA Modules:
  0.0 36.9 jit_solution(3917353696341885535)
XLA Ops:
  0.6 34.6 %pose_solve.1.result = f32[88,128]{1,0:T(8,128)} custom-call(f32[1,48]{1,0:T(1,128)} %bitcast.6, s32[1,64]{1,0:T(1,128)} %bitcast.7, bf16[64,48,128]{2,1,0:T(8,128)(2,1)} %enc_in.1, f32[3,64]{1,0:T(4,128)} %bitcast.4, bf16[4,128,128]{2,1,0:T(8,128)(2,1)} %w_in.1, bf16[3,128]{1,0:T(4,128)(2,1)} %bitcast.5, f32[38,128]{1,0:T(8,128)} %lift_in.1, ...), custom_call_target="tpu_custom_call" | custom-call | tf_op jit(solution)/shard_map/pose_solve/pallas_call | solution.py:343
  35.2 1.6 %pose_place.1 = (f32[38,256]{1,0:T(8,128)}, f32[38,256]{1,0:T(8,128)}) custom-call(f32[88,128]{1,0:T(8,128)} %pose_solve.1.result), custom_call_target="tpu_custom_call" | custom-call | tf_op jit(solution)/shard_map/pose_place/pallas_call | solution.py:383

commit v4 on v3

--- a/solution.py
+++ b/solution.py
@@ -76,6 +76,17 @@
     return jnp.concatenate([high, middle, low], axis=0)
 
 
+def two_terms(a, axis):
+    high = a.astype(B)
+    return jnp.concatenate([high, (a - high.astype(F)).astype(B)], axis=axis)
+
+
+def dot_two(a, b, dims):
+    out = dot(a, b, dims, None)
+    m, n = out.shape[0] // 2, out.shape[1] // 2
+    return (out[0:m, 0:n] + (out[0:m, n:] + out[m:, 0:n])) + out[m:, n:]
+
+
 def dot_terms(terms, b, dims):
     n = terms.shape[0] // 3
     out = dot(terms, b, dims, None)
@@ -139,7 +150,7 @@
 def kernel(
     quad_in, ids_in, enc_in, targets_in, w_in, hw_in, lift_in, params_in, damping_in,
     result_out,
-    enc, targets, w, hw_b, lift_b, quad_b, wt, lift, quad, ids, owned, owned_damping,
+    enc, targets, w, hw_b, lift_b, quad_b, wt, lift, lift2, quad, ids, owned, owned_damping,
     reply, reply_damping, columns, columns_damping, grads, mixed, tiles, turned,
     load_sem, send_sem, recv_sem, group_sem,
 ):
@@ -192,6 +203,7 @@
     for load in loads[3:8]:
         load.wait()
     lift[0:PARAMS] = lift_b[...]
+    lift2[...] = two_terms(lift[...], 0)
     quad[...] = jnp.broadcast_to(quad_b[...], (D, SAMPLES)).T
     hw = hw_b[...].astype(F)
     wait(ids.at[pl.ds(0, OWN)], recv_sem.at[0])
@@ -243,13 +255,11 @@
     residual = dot(hw, mixed[...], ((1,), (1,))) - targets[...]
     lane8 = lax.broadcasted_iota(jnp.int32, (8, D), 1)
     sub8 = lax.broadcasted_iota(jnp.int32, (8, D), 0)
-    rows = dot(grads[...].reshape(COLORS * RAYS, D), lift[...], ((1,), (1,)))
-    matrix = dot(rows.T[0:40], rows, ((1,), (0,)))
-    right = jnp.zeros((1, D), F)
-    for c in range(COLORS):
-        part = rows[c * RAYS : (c + 1) * RAYS]
-        right = right - dot(residual[c : c + 1], part, ((1,), (0,)))
-    right = jnp.broadcast_to(right, (8, D))
+    rows = dot_two(two_terms(grads[...].reshape(COLORS * RAYS, D), 0), lift2[...], ((1,), (1,)))
+    residual = jnp.concatenate([residual[c : c + 1] for c in range(COLORS)], axis=1)
+    left = jnp.concatenate([rows.T[0:40], jnp.broadcast_to(-residual, (8, COLORS * RAYS))], axis=0)
+    matrix = dot_two(two_terms(left, 0), two_terms(rows, 1), ((1,), (0,)))
+    right = matrix[40:48]
     camera = ids[OWN][:, 0:1].astype(F)
     damp = jnp.where(lane8 == PARAMS, camera, jnp.broadcast_to(damp, (8, D)))
     out = jnp.zeros((8, D), F)
@@ -340,6 +350,10 @@
 def body(encodings, ray_camera, targets, weights, head_weight, quadrature, lift, cam_params, damping):
     vmem = pl.BlockSpec(memory_space=pltpu.VMEM)
     hbm = pl.BlockSpec(memory_space=pl.ANY)
+    inputs = (
+        quadrature.reshape(1, SAMPLES), ray_camera.reshape(1, RAYS), encodings, targets.T, weights,
+        head_weight.T, lift, cam_params, damping,
+    )
     result = pl.pallas_call(
         kernel,
         out_shape=jax.ShapeDtypeStruct((88, N), F),
@@ -354,6 +368,7 @@
             pltpu.VMEM((1, SAMPLES), F),
             pltpu.VMEM((LAYERS, D, D), B),
             pltpu.VMEM((D, D), F),
+            pltpu.VMEM((2 * D, D), B),
             pltpu.VMEM((SAMPLES, D), F),
             pltpu.VMEM((ASKERS, 1, RAYS), jnp.int32),
             pltpu.VMEM((4, PARAMS, COLS), F),
@@ -373,15 +388,15 @@
         ],
         name="pose_solve",
         compiler_params=pltpu.CompilerParams(
-            collective_id=0, has_side_effects=True, vmem_limit_bytes=60 * 2**20
+            collective_id=0, has_side_effects=True, vmem_limit_bytes=48 * 2**20
         ),
     )(
-        quadrature.reshape(1, SAMPLES), ray_camera.reshape(1, RAYS), encodings, targets.T, weights, head_weight.T, lift,
-        cam_params, damping,
+        *(pltpu.with_memory_space_constraint(x, pltpu.HBM) for x in inputs)
     )
     out = jax.ShapeDtypeStruct((PARAMS, COLS), F)
     return pl.pallas_call(
-        place, out_shape=(out, out), in_specs=[vmem], out_specs=(vmem, vmem), name="pose_place"
+        place, out_shape=(out, out), in_specs=[vmem], out_specs=(vmem, vmem), name="pose_place",
+        compiler_params=pltpu.CompilerParams(vmem_limit_bytes=8 * 2**20),
     )(result)
 
 

time: 37 us -> 35.3 us (0.954)
  Pallas kernels: 36.2 us -> 34.5 us
    pallas_call x1, Pallas kernels: 34.6 us -> 33.7 us  [body(): pl.pallas_call(kernel, out_shape=jax.ShapeDtypeStruct((88, N), F), in_spe...]
    pallas_call x1, Pallas kernels: 1.63 us -> 0.83 us  [body(): pl.pallas_call(place, out_shape=(out, out), in_specs=[vmem], out_specs=(v...]
where the time goes in v4:
time: 35.3 us; the launch traced here: 35.1 us
  Pallas kernels  34.5 us (98%)
  between operations  0.64 us (2%)
    pallas_call x1, Pallas kernels, body(): pl.pallas_call(kernel, out_shape=jax.ShapeDtypeStruct((88, N), F), in_spe...  33.7 us
    pallas_call x1, Pallas kernels, body(): pl.pallas_call(place, out_shape=(out, out), in_specs=[vmem], out_specs=(v...  0.83 us

profile of v4, /device:TPU:1, one launch (start us, length us, event | category | flops | bytes accessed | tf_op | source)
XLA Modules:
  0.0 35.1 jit_solution(16839251119304492941)
XLA Ops:
  0.6 33.7 %pose_solve.1.result = f32[88,128]{1,0:T(8,128)S(1)} custom-call(f32[1,48]{1,0:T(1,128)} %bitcast.6, s32[1,64]{1,0:T(1,128)} %bitcast.7, bf16[64,48,128]{2,1,0:T(8,128)(2,1)} %enc_in.1, f32[3,64]{1,0:T(4,128)} %bitcast.4, bf16[4,128,128]{2,1,0:T(8,128)(2,1)} %w_in.1, bf16[3,128]{1,0:T(4,128)(2,1)} %bitcast.5, f32[38,128]{1,0:T(8,128)} %lift_in.1, ...), custom_call_target="tpu_custom_call" | custom-call | tf_op jit(solution)/shard_map/pose_solve/pallas_call | solution.py:357
  34.3 0.8 %pose_place.1 = (f32[38,256]{1,0:T(8,128)}, f32[38,256]{1,0:T(8,128)}) custom-call(f32[88,128]{1,0:T(8,128)S(1)} %pose_solve.1.result), custom_call_target="tpu_custom_call" | custom-call | tf_op jit(solution)/shard_map/pose_place/pallas_call | solution.py:397

commit v5 on v4

--- a/solution.py
+++ b/solution.py
@@ -164,7 +164,7 @@
         pltpu.make_async_copy(ref, ref, sem).wait()
 
     barrier = pltpu.get_barrier_semaphore()
-    for o in ROWS + COLUMN + LINE:
+    for o in [opposite(PLANE[i]) for i in ANSWERED] + LINE:
         pl.semaphore_signal(barrier, inc=1, device_id=device(o), device_id_type=MESH)
     loads = [
         pltpu.make_async_copy(source, target, load_sem.at[i])
@@ -191,10 +191,10 @@
     depth = (lax.broadcasted_iota(jnp.int32, (SAMPLES, D), 0).astype(F) + 1.0) / SAMPLES
     loads[0].wait()
     loads[1].wait()
-    pl.semaphore_wait(barrier, len(ROWS) + len(COLUMN) + len(LINE))
-
-    for i, o in enumerate(ROWS):
-        send(ids.at[OWN], ids.at[i], 0, o)
+    pl.semaphore_wait(barrier, len(ANSWERED) + len(LINE))
+
+    for i in ANSWERED:
+        send(ids.at[OWN], ids.at[i], 0, PLANE[i])
     for o in LINE:
         send(owned.at[0], owned.at[o[3]], 1, o)
     loads[2].wait()
@@ -206,10 +206,6 @@
     lift2[...] = two_terms(lift[...], 0)
     quad[...] = jnp.broadcast_to(quad_b[...], (D, SAMPLES)).T
     hw = hw_b[...].astype(F)
-    wait(ids.at[pl.ds(0, OWN)], recv_sem.at[0])
-    row = ids.at[pl.ds(0, OWN + 1)]
-    for o in COLUMN:
-        send(row, ids.at[pl.ds(o[0] * (OWN + 1), OWN + 1)], 7, o)
     for layer in range(LAYERS):
         wt[layer] = w[layer].T
 
@@ -219,7 +215,7 @@
 
     wait(owned.at[pl.ds(1, 3)], recv_sem.at[1])
     terms = terms_of(owned)
-    wait(ids.at[pl.ds(OWN + 1, 3 * (OWN + 1))], recv_sem.at[7])
+    wait(ids.at[pl.ds(0, ASKERS - 1)], recv_sem.at[0])
 
     asked = ids[...].reshape(ASKERS, RAYS).astype(F)
     here = lax.broadcasted_iota(jnp.int32, (ASKERS, RAYS), 0) == lax.broadcasted_iota(
@@ -328,8 +324,7 @@
     result_out[0:40] = answered * once
     result_out[40:80] = remainder * once
     result_out[80:88] = jnp.broadcast_to(id_lanes, (8, N))
-    wait(ids.at[pl.ds(0, OWN)], send_sem.at[0])
-    wait(ids.at[pl.ds(OWN + 1, 3 * (OWN + 1))], send_sem.at[7])
+    wait(ids.at[pl.ds(0, ASKERS - 1)], send_sem.at[0])
     wait(owned.at[pl.ds(1, 3)], send_sem.at[1])
     wait(owned_damping.at[pl.ds(1, 3)], send_sem.at[2])
     wait(columns.at[pl.ds(0, ASKERS - 1)], send_sem.at[3])

time: 35.3 us -> 34.7 us (0.983)
  Pallas kernels: 34.5 us -> 34 us
    pallas_call x1, Pallas kernels: 33.7 us -> 33.1 us  [body(): pl.pallas_call(kernel, out_shape=jax.ShapeDtypeStruct((88, N), F), in_spe...]
where the time goes in v5:
time: 34.7 us; the launch traced here: 34.6 us
  Pallas kernels  34 us (98%)
  between operations  0.64 us (2%)
    pallas_call x1, Pallas kernels, body(): pl.pallas_call(kernel, out_shape=jax.ShapeDtypeStruct((88, N), F), in_spe...  33.1 us
    pallas_call x1, Pallas kernels, body(): pl.pallas_call(place, out_shape=(out, out), in_specs=[vmem], out_specs=(v...  0.84 us

profile of v5, /device:TPU:1, one launch (start us, length us, event | category | flops | bytes accessed | tf_op | source)
XLA Modules:
  0.0 34.6 jit_solution(2819358019190777981)
XLA Ops:
  0.6 33.1 %pose_solve.1.result = f32[88,128]{1,0:T(8,128)S(1)} custom-call(f32[1,48]{1,0:T(1,128)} %bitcast.6, s32[1,64]{1,0:T(1,128)} %bitcast.7, bf16[64,48,128]{2,1,0:T(8,128)(2,1)} %enc_in.1, f32[3,64]{1,0:T(4,128)} %bitcast.4, bf16[4,128,128]{2,1,0:T(8,128)(2,1)} %w_in.1, bf16[3,128]{1,0:T(4,128)(2,1)} %bitcast.5, f32[38,128]{1,0:T(8,128)} %lift_in.1, ...), custom_call_target="tpu_custom_call" | custom-call | tf_op jit(solution)/shard_map/pose_solve/pallas_call | solution.py:352
  33.8 0.8 %pose_place.1 = (f32[38,256]{1,0:T(8,128)}, f32[38,256]{1,0:T(8,128)}) custom-call(f32[88,128]{1,0:T(8,128)S(1)} %pose_solve.1.result), custom_call_target="tpu_custom_call" | custom-call | tf_op jit(solution)/shard_map/pose_place/pallas_call | solution.py:392

commit v6 on v5

--- a/solution.py
+++ b/solution.py
@@ -197,10 +197,7 @@
         send(ids.at[OWN], ids.at[i], 0, PLANE[i])
     for o in LINE:
         send(owned.at[0], owned.at[o[3]], 1, o)
-    loads[2].wait()
-    for o in LINE:
-        send(owned_damping.at[0], owned_damping.at[o[3]], 2, o)
-    for load in loads[3:8]:
+    for load in loads[2:8]:
         load.wait()
     lift[0:PARAMS] = lift_b[...]
     lift2[...] = two_terms(lift[...], 0)
@@ -214,6 +211,8 @@
         return three_terms(jnp.concatenate([wide, jnp.zeros((2, 4 * COLS), F)], axis=0))
 
     wait(owned.at[pl.ds(1, 3)], recv_sem.at[1])
+    for o in LINE:
+        send(owned_damping.at[0], owned_damping.at[o[3]], 2, o)
     terms = terms_of(owned)
     wait(ids.at[pl.ds(0, ASKERS - 1)], recv_sem.at[0])
 

time: 34.7 us -> 33.7 us (0.971)
  Pallas kernels: 34 us -> 32.9 us
    pallas_call x1, Pallas kernels: 33.1 us -> 32.1 us  [body(): pl.pallas_call(kernel, out_shape=jax.ShapeDtypeStruct((88, N), F), in_spe...]
where the time goes in v6:
time: 33.7 us; the launch traced here: 33.6 us
  Pallas kernels  32.9 us (98%)
  between operations  0.64 us (2%)
    pallas_call x1, Pallas kernels, body(): pl.pallas_call(kernel, out_shape=jax.ShapeDtypeStruct((88, N), F), in_spe...  32.1 us
    pallas_call x1, Pallas kernels, body(): pl.pallas_call(place, out_shape=(out, out), in_specs=[vmem], out_specs=(v...  0.84 us

profile of v6, /device:TPU:1, one launch (start us, length us, event | category | flops | bytes accessed | tf_op | source)
XLA Modules:
  0.0 33.6 jit_solution(16589977693401225781)
XLA Ops:
  0.6 32.1 %pose_solve.1.result = f32[88,128]{1,0:T(8,128)S(1)} custom-call(f32[1,48]{1,0:T(1,128)} %bitcast.6, s32[1,64]{1,0:T(1,128)} %bitcast.7, bf16[64,48,128]{2,1,0:T(8,128)(2,1)} %enc_in.1, f32[3,64]{1,0:T(4,128)} %bitcast.4, bf16[4,128,128]{2,1,0:T(8,128)(2,1)} %w_in.1, bf16[3,128]{1,0:T(4,128)(2,1)} %bitcast.5, f32[38,128]{1,0:T(8,128)} %lift_in.1, ...), custom_call_target="tpu_custom_call" | custom-call | tf_op jit(solution)/shard_map/pose_solve/pallas_call | solution.py:351
  32.7 0.8 %pose_place.1 = (f32[38,256]{1,0:T(8,128)}, f32[38,256]{1,0:T(8,128)}) custom-call(f32[88,128]{1,0:T(8,128)S(1)} %pose_solve.1.result), custom_call_target="tpu_custom_call" | custom-call | tf_op jit(solution)/shard_map/pose_place/pallas_call | solution.py:391
